TPU v7x, 128 devices: a whole 4x4x4 slice. The times are simulated.
128 devices in a mesh: seq: 64 (over x, y_lo, z, core), grp: 2 (over y_hi).
Axes of the slice: x: 4, y: 4 (y_hi: 2, y_lo: 2; y = y_hi * 2 + y_lo), z: 4, core: 2. Of those that a mesh axis runs over, the one named last changes fastest.
Arguments:
- enc_q: bfloat16 [8192, 2048], P('seq', 'grp'), may hold values from -32 to 32
- enc_k: bfloat16 [8192, 2048], P('seq', 'grp'), may hold values from -32 to 32
- enc_v: bfloat16 [8192, 2048], P('seq', 'grp'), may hold values from -6 to 6
- enc_cot: bfloat16 [8192, 2048], P('seq', 'grp'), may hold values from -1.5 to 1.5
- cross_k: bfloat16 [8192, 2048], P('seq', 'grp'), may hold values from -32 to 32
- cross_v: bfloat16 [8192, 2048], P('seq', 'grp'), may hold values from -6 to 6
- dec_q: bfloat16 [2048, 2048], P(('seq', 'grp')), may hold values from -32 to 32
- dec_cot: bfloat16 [2048, 2048], P(('seq', 'grp')), may hold values from -1.5 to 1.5
- frame_lengths: int32 [64], replicated, may hold values from 64 to 128
Outputs:
- enc_out: bfloat16 [8192, 2048], P('seq', 'grp')
- enc_dq: bfloat16 [8192, 2048], P('seq', 'grp')
- enc_dk: bfloat16 [8192, 2048], P('seq', 'grp')
- enc_dv: bfloat16 [8192, 2048], P('seq', 'grp')
- dec_out: bfloat16 [2048, 2048], P(('seq', 'grp'))
- dec_dq: bfloat16 [2048, 2048], P(('seq', 'grp'))
- cross_dk: bfloat16 [8192, 2048], P('seq', 'grp')
- cross_dv: bfloat16 [8192, 2048], P('seq', 'grp')
All inputs are finite; a program needn't handle non-finite values.
Results may differ from a plain program's by a relative error of at most 0.04.
Values may be sent and summed in bfloat16 or wider, within the bound.
A program may use at most 128 MiB of HBM per device.

v0:
```python
import functools
import math

import jax
import jax.numpy as jnp
from jax import lax
from jax.experimental import pallas as pl
from jax.experimental.pallas import tpu as pltpu
from jax.sharding import PartitionSpec as P

HD = 128
FB = 128
TB = 16
SCALE = HD ** (-0.5)
C2 = SCALE * math.log2(math.e)
NEG = -1e30
F32 = jnp.float32
BF16 = jnp.bfloat16
MESH = pl.DeviceIdType.MESH


def nt(a, b):
    return lax.dot_general(a, b, (((1,), (1,)), ((), ())), preferred_element_type=F32)


def nn(a, b):
    return lax.dot_general(a, b, (((1,), (0,)), ((), ())), preferred_element_type=F32)


def drain(ref, sem):
    pltpu.make_async_copy(ref, ref, sem).wait()


def lanes(column, width):
    return column if width == HD else jnp.concatenate([column] * (width // HD), axis=1)


def kernel(
    G, NF, len_ref, eq, ek, ev, ec, ckh, cvh, dqh, dch,
    o_eo, o_edq, o_edk, o_edv, o_do, o_ddq, o_cdk, o_cdv,
    eqb, ecb, ekb, evb, ekT, evT, ckb, cvb, ckT, cvT, qt, ct, pbuf, sbuf, wbuf, dsbuf,
    bias, nsend, nrecv, ssend, srecv, stat, dqsend, dqrecv,
    eos, edqs, edks, edvs, eka, eva, cka, cva, gsend, grecv, cdks, cdvs, toko, tokdq,
    sem_in, sem_halo, sem_tok, sem_num, sem_st, sem_stat, sem_dq, sem_grad, sem_out, sem_send,
):
    R = G // 2
    TC = 2 * TB * G
    W = 2 * FB
    s = lax.axis_index("seq")
    g = lax.axis_index("grp")
    f = lax.div(s, G)
    r = lax.rem(s, G)
    col = pl.ds(pl.multiple_of(r * HD, HD), HD)

    def send(src, dst, ssem, rsem, ts, tg):
        pltpu.make_async_remote_copy(
            src_ref=src, dst_ref=dst, send_sem=ssem, recv_sem=rsem,
            device_id=(ts, tg), device_id_type=MESH,
        ).start()

    def cols(ref, head):
        return ref.at[:, pl.ds(pl.multiple_of(head * HD, HD), HD)]

    def rows(ref, index, size):
        return ref.at[pl.ds(pl.multiple_of(index * size, size), size), :]

    pltpu.make_async_copy(cols(ckh, r), rows(ckb, r, FB), sem_in.at[0]).start()
    pltpu.make_async_copy(cols(cvh, r), rows(cvb, r, FB), sem_in.at[1]).start()
    pltpu.make_async_copy(cols(ek, r), rows(ekb, R + r, FB), sem_in.at[2]).start()
    pltpu.make_async_copy(cols(ev, r), rows(evb, R + r, FB), sem_in.at[3]).start()
    pltpu.make_async_copy(cols(eq, r), rows(eqb, r, FB), sem_in.at[4]).start()
    pltpu.make_async_copy(cols(ec, r), rows(ecb, r, FB), sem_in.at[5]).start()
    place = r * 2 + g
    own_tok = f * (2 * G) + place
    pltpu.make_async_copy(cols(dqh, g * G + r), rows(qt, own_tok, TB), sem_tok.at[0, f]).start()
    pltpu.make_async_copy(cols(dch, g * G + r), rows(ct, own_tok, TB), sem_tok.at[1, f]).start()

    barrier = pltpu.get_barrier_semaphore()

    def greet(ts, tg):
        pl.semaphore_signal(barrier, inc=1, device_id=(ts, tg), device_id_type=MESH)

    for n in range(1, G):
        greet(f * G + lax.rem(r + n, G), g)
    for n in range(G):
        greet(f * G + n, 1 - g)
    for n in range(1, NF):
        greet(lax.rem(f + n, NF) * G + r, g)

    @pl.when(f > 0)
    def _():
        for n in range(1, G):
            greet((f - 1) * G + lax.rem(r + n, G), g)

    @pl.when(f < NF - 1)
    def _():
        for n in range(1, G):
            greet((f + 1) * G + lax.rem(r + n, G), g)

    row = lax.broadcasted_iota(jnp.int32, (FB, HD), 0)
    for blk in range(2 * G):
        gb = f * G - R + blk
        length = len_ref[jnp.clip(gb, 0, NF * G - 1)]
        length = jnp.where((gb >= 0) & (gb < NF * G), length, 0)
        bias[blk * FB:(blk + 1) * FB, :] = jnp.where(row < length, 0.0, NEG).astype(F32)
    zero = jnp.zeros((R * FB, HD), BF16)

    @pl.when(f == 0)
    def _():
        ekb[0:R * FB, :] = zero
        evb[0:R * FB, :] = zero

    @pl.when(f == NF - 1)
    def _():
        ekb[(R + G) * FB:, :] = zero
        evb[(R + G) * FB:, :] = zero

    eka[...] = jnp.zeros(eka.shape, F32)
    eva[...] = jnp.zeros(eva.shape, F32)
    cka[...] = jnp.zeros(cka.shape, F32)
    cva[...] = jnp.zeros(cva.shape, F32)

    sides = jnp.where(f > 0, 1, 0) + jnp.where(f < NF - 1, 1, 0)
    pl.semaphore_wait(barrier, (G - 1) + G + (NF - 1) + sides * (G - 1))

    for n in range(1, 2 * G):
        to = lax.rem(place + n, 2 * G)
        tr, tg = lax.div(to, 2), lax.rem(to, 2)
        send(cols(dqh, tg * G + tr), rows(qt, own_tok, TB), sem_send.at[0], sem_tok.at[0, f], f * G + tr, tg)
        send(cols(dch, tg * G + tr), rows(ct, own_tok, TB), sem_send.at[1], sem_tok.at[1, f], f * G + tr, tg)
    for n in range(1, G):
        p = lax.rem(r + n, G)
        send(cols(ckh, p), rows(ckb, r, FB), sem_send.at[2], sem_in.at[0], f * G + p, g)
        send(cols(cvh, p), rows(cvb, r, FB), sem_send.at[3], sem_in.at[1], f * G + p, g)
    for n in range(1, G):
        p = lax.rem(r + n, G)
        send(cols(ek, p), rows(ekb, R + r, FB), sem_send.at[4], sem_in.at[2], f * G + p, g)
        send(cols(eq, p), rows(eqb, r, FB), sem_send.at[6], sem_in.at[4], f * G + p, g)
        send(cols(ev, p), rows(evb, R + r, FB), sem_send.at[5], sem_in.at[3], f * G + p, g)
        send(cols(ec, p), rows(ecb, r, FB), sem_send.at[7], sem_in.at[5], f * G + p, g)
    late = lax.div(r, R)
    fh = f - 1 + 2 * late
    slot = lax.rem(r + G + R, 2 * G) * (1 - late) + (r - R) * late
    has_halo = (fh >= 0) & (fh < NF)

    @pl.when(has_halo)
    def _():
        for n in range(G):
            p = lax.rem(r + n, G)
            send(cols(ek, p), rows(ekb, slot, FB), sem_send.at[8], sem_halo.at[0, late], fh * G + p, g)
            send(cols(ev, p), rows(evb, slot, FB), sem_send.at[9], sem_halo.at[1, late], fh * G + p, g)

    drain(rows(qt, f, TC), sem_tok.at[0, f])
    drain(rows(ct, f, TC), sem_tok.at[1, f])
    for n in range(1, NF):
        to = lax.rem(f + n, NF)
        send(rows(qt, f, TC), rows(qt, f, TC), sem_send.at[10], sem_tok.at[0, f], to * G + r, g)
    for n in range(1, NF):
        to = lax.rem(f + n, NF)
        send(rows(ct, f, TC), rows(ct, f, TC), sem_send.at[11], sem_tok.at[1, f], to * G + r, g)

    row8 = lax.broadcasted_iota(jnp.int32, (8, TC), 0)

    def pack(a, b, c):
        return jnp.where(row8 == 0, a, jnp.where(row8 == 1, b, c))

    drain(ckb, sem_in.at[0])
    drain(cvb, sem_in.at[1])
    cvT[...] = cvb[...].T
    ckT[...] = ckb[...].T

    def cross_forward(t):
        q = qt[pl.ds(pl.multiple_of(t * TC, TC), TC), :]
        top = None
        for u in range(G // 2):
            part = nt(ckb[u * W:(u + 1) * W, :], q)
            part = part + lanes(bias[(R * FB) + u * W:(R * FB) + (u + 1) * W, :], TC)
            sbuf[u * W:(u + 1) * W, 0:TC] = part
            high = jnp.max(part, axis=0, keepdims=True)
            top = high if top is None else jnp.maximum(top, high)
        total = jnp.zeros((1, TC), F32)
        for u in range(G // 2):
            expo = jnp.exp2((sbuf[u * W:(u + 1) * W, 0:TC] - top) * C2)
            total = total + jnp.sum(expo, axis=0, keepdims=True)
            pbuf[t, u * W:(u + 1) * W, :] = expo.astype(BF16)
        numer = nn(cvT[...], pbuf[t])
        nsend[t] = numer.astype(BF16)
        ssend[t] = pack(top, total, total)

    cross_forward(f)
    nrecv[f] = nsend[f]
    srecv[f] = ssend[f]

    @pl.loop(1, NF)
    def _(i):
        t = lax.rem(f + i, NF)
        drain(rows(qt, t, TC), sem_tok.at[0, t])
        cross_forward(t)
        send(nsend.at[t], nrecv.at[f], sem_send.at[12], sem_num, t * G + r, g)
        send(ssend.at[t], srecv.at[f], sem_send.at[13], sem_st, t * G + r, g)

    drain(rows(ekb, 0, G * FB), sem_in.at[2])
    drain(rows(evb, 0, G * FB), sem_in.at[3])
    drain(eqb, sem_in.at[4])
    drain(ecb, sem_in.at[5])

    @pl.when(f > 0)
    def _():
        drain(rows(ekb, 0, R * FB), sem_halo.at[0, 1])
        drain(rows(evb, 0, R * FB), sem_halo.at[1, 1])

    @pl.when(f < NF - 1)
    def _():
        drain(rows(ekb, 0, R * FB), sem_halo.at[0, 0])
        drain(rows(evb, 0, R * FB), sem_halo.at[1, 0])

    ekT[...] = ekb[...].T
    evT[...] = evb[...].T

    NU = (G + 2) // 2
    urow = lax.broadcasted_iota(jnp.int32, (W, W), 0)
    ulane = lax.broadcasted_iota(jnp.int32, (W, W), 1)

    def encoder_pair(j):
        base = pl.multiple_of(j * W, W)
        q = eqb[pl.ds(base, W), :]
        cot = ecb[pl.ds(base, W), :]
        top = None
        for u in range(NU):
            at = pl.multiple_of(base + u * W, W)
            part = nt(ekb[pl.ds(at, W), :], q) + lanes(bias[pl.ds(at, W), :], W)
            if u == 0:
                part = jnp.where((urow < FB) & (ulane >= FB), NEG, part)
            if u == NU - 1:
                part = jnp.where((urow >= FB) & (ulane < FB), NEG, part)
            sbuf[u * W:(u + 1) * W, :] = part
            high = jnp.max(part, axis=0, keepdims=True)
            top = high if top is None else jnp.maximum(top, high)
        total = jnp.zeros((1, W), F32)
        for u in range(NU):
            expo = jnp.exp2((sbuf[u * W:(u + 1) * W, :] - top) * C2)
            total = total + jnp.sum(expo, axis=0, keepdims=True)
            sbuf[u * W:(u + 1) * W, :] = expo
            wbuf[u * W:(u + 1) * W, :] = expo.astype(BF16)
        numer = nn(evT[:, pl.ds(base, NU * W)], wbuf[...])
        out = (numer / total).astype(BF16).astype(F32)
        delta = jnp.sum(cot.astype(F32).T * out, axis=0, keepdims=True)
        eos[pl.ds(base, W), :] = out.T.astype(BF16)
        inv = 1.0 / total
        for u in range(NU):
            at = pl.multiple_of(base + u * W, W)
            prob = sbuf[u * W:(u + 1) * W, :] * inv
            dprob = nt(evb[pl.ds(at, W), :], cot)
            ds = (prob * (dprob - delta)).astype(BF16)
            dsbuf[u * W:(u + 1) * W, :] = ds
            eka[pl.ds(at, W), :] += nn(ds, q)
            eva[pl.ds(at, W), :] += nn(prob.astype(BF16), cot)
        dq = nn(ekT[:, pl.ds(base, NU * W)], dsbuf[...]) * SCALE
        edqs[pl.ds(base, W), :] = dq.T.astype(BF16)
        for half in range(2):
            b = 2 * j + half

            @pl.when(b != r)
            def _():
                send(rows(eos, b, FB), o_eo.at[:, col], sem_send.at[14], sem_out.at[0], f * G + b, g)
                send(rows(edqs, b, FB), o_edq.at[:, col], sem_send.at[15], sem_out.at[1], f * G + b, g)

            @pl.when(b == r)
            def _():
                pltpu.make_async_copy(rows(eos, b, FB), o_eo.at[:, col], sem_out.at[0]).start()
                pltpu.make_async_copy(rows(edqs, b, FB), o_edq.at[:, col], sem_out.at[1]).start()

    def chunk_home(src, dst, k):
        mine = pl.ds(pl.multiple_of((g * G + r) * HD, HD), HD)
        for n in range(1, 2 * G):
            to = lax.rem(place + n, 2 * G)
            tr, tg = lax.div(to, 2), lax.rem(to, 2)
            send(rows(src, to, TB), dst.at[:, mine], sem_send.at[k], sem_out.at[k - 12], f * G + tr, tg)
        pltpu.make_async_copy(rows(src, place, TB), dst.at[:, mine], sem_out.at[k - 12]).start()

    encoder_pair(0)

    drain(nrecv.at[0:NF - 1], sem_num)
    drain(srecv.at[0:NF - 1], sem_st)
    top = srecv[0, 0:1, :]
    for n in range(1, NF):
        top = jnp.maximum(top, srecv[n, 0:1, :])
    total = jnp.zeros((1, TC), F32)
    numer = jnp.zeros((HD, TC), F32)
    for n in range(NF):
        share = jnp.exp2((srecv[n, 0:1, :] - top) * C2)
        total = total + share * srecv[n, 1:2, :]
        numer = numer + share * nrecv[n].astype(F32)
    out = (numer / total).astype(BF16).astype(F32)
    cot = ct[pl.ds(pl.multiple_of(f * TC, TC), TC), :]
    delta = jnp.sum(cot.astype(F32).T * out, axis=0, keepdims=True)
    toko[...] = out.T.astype(BF16)
    stat[f] = pack(top, 1.0 / total, delta)
    for n in range(1, NF):
        to = lax.rem(f + n, NF)
        send(stat.at[f], stat.at[f], sem_send.at[18], sem_stat.at[f], to * G + r, g)
    chunk_home(toko, o_do, 16)

    @pl.loop(1, G // 2)
    def _(j):
        encoder_pair(j)

    @pl.when(f > 0)
    def _():
        gsend[0, 0] = (eka[0:R * FB, :] * SCALE).astype(BF16)
        gsend[0, 1] = eva[0:R * FB, :].astype(BF16)
        send(gsend.at[0], grecv.at[1], sem_send.at[19], sem_grad.at[1], (f - 1) * G + r, g)

    @pl.when(f < NF - 1)
    def _():
        gsend[1, 0] = (eka[(R + G) * FB:, :] * SCALE).astype(BF16)
        gsend[1, 1] = eva[(R + G) * FB:, :].astype(BF16)
        send(gsend.at[1], grecv.at[0], sem_send.at[20], sem_grad.at[0], (f + 1) * G + r, g)

    def cross_backward(t):
        at = pl.ds(pl.multiple_of(t * TC, TC), TC)
        q = qt[at, :]
        cot = ct[at, :]
        share = jnp.exp2((ssend[t, 0:1, :] - stat[t, 0:1, :]) * C2) * stat[t, 1:2, :]
        delta = stat[t, 2:3, :]
        for u in range(G // 2):
            here = slice(u * W, (u + 1) * W)
            prob = pbuf[t, u * W:(u + 1) * W, :].astype(F32) * share
            dprob = nt(cvb[here, :], cot)
            ds = (prob * (dprob - delta)).astype(BF16)
            dsbuf[here, 0:TC] = ds
            cka[here, :] += nn(ds, q)
            cva[here, :] += nn(prob.astype(BF16), cot)
        dqsend[t] = nn(ckT[...], dsbuf[0:G * FB, 0:TC]).astype(BF16)

    def backward_step(i):
        t = lax.rem(f + i, NF)
        drain(rows(ct, t, TC), sem_tok.at[1, t])
        drain(stat.at[t], sem_stat.at[t])
        cross_backward(t)
        send(dqsend.at[t], dqrecv.at[f], sem_send.at[21], sem_dq, t * G + r, g)

    @pl.loop(1, NF // 2 + 1)
    def _(i):
        backward_step(i)

    own = slice(R * FB, (R + G) * FB)
    edks[...] = (eka[own, :] * SCALE).astype(BF16)
    edvs[...] = eva[own, :].astype(BF16)

    @pl.when(f > 0)
    def _():
        drain(grecv.at[0], sem_grad.at[0])
        edks[0:R * FB, :] = (eka[R * FB:2 * R * FB, :] * SCALE + grecv[0, 0].astype(F32)).astype(BF16)
        edvs[0:R * FB, :] = (eva[R * FB:2 * R * FB, :] + grecv[0, 1].astype(F32)).astype(BF16)

    @pl.when(f < NF - 1)
    def _():
        drain(grecv.at[1], sem_grad.at[1])
        edks[R * FB:, :] = (eka[2 * R * FB:3 * R * FB, :] * SCALE + grecv[1, 0].astype(F32)).astype(BF16)
        edvs[R * FB:, :] = (eva[2 * R * FB:3 * R * FB, :] + grecv[1, 1].astype(F32)).astype(BF16)

    def heads_home(src, dst, ks, ko):
        for n in range(1, G):
            p = lax.rem(r + n, G)
            send(rows(src, p, FB), dst.at[:, col], sem_send.at[ks], sem_out.at[ko], f * G + p, g)
        pltpu.make_async_copy(rows(src, r, FB), dst.at[:, col], sem_out.at[ko]).start()

    heads_home(edks, o_edk, 22, 2)
    heads_home(edvs, o_edv, 23, 3)

    @pl.loop(NF // 2 + 1, NF)
    def _(i):
        backward_step(i)

    cross_backward(f)
    dqrecv[f] = dqsend[f]
    cdks[...] = (cka[...] * SCALE).astype(BF16)
    heads_home(cdks, o_cdk, 24, 6)
    cdvs[...] = cva[...].astype(BF16)
    heads_home(cdvs, o_cdv, 25, 7)
    drain(dqrecv.at[0:NF - 1], sem_dq)
    dq = dqrecv[0].astype(F32)
    for n in range(1, NF):
        dq = dq + dqrecv[n].astype(F32)
    tokdq[...] = (dq * SCALE).T.astype(BF16)
    chunk_home(tokdq, o_ddq, 17)

    for k, ref in enumerate((o_eo, o_edq, o_edk, o_edv, o_do, o_ddq, o_cdk, o_cdv)):
        drain(ref, sem_out.at[k])
    others = eqb.at[0:(G - 1) * FB, :]
    tokens = qt.at[0:(2 * G - 1) * TB, :]
    drain(tokens, sem_send.at[0])
    drain(tokens, sem_send.at[1])
    for k in (2, 3, 4, 5, 6, 7, 14, 15, 22, 23, 24, 25):
        drain(others, sem_send.at[k])

    @pl.when(has_halo)
    def _():
        drain(eqb, sem_send.at[8])
        drain(eqb, sem_send.at[9])

    drain(qt.at[0:(NF - 1) * TC, :], sem_send.at[10])
    drain(qt.at[0:(NF - 1) * TC, :], sem_send.at[11])
    drain(nrecv.at[0:NF - 1], sem_send.at[12])
    drain(srecv.at[0:NF - 1], sem_send.at[13])
    drain(tokens, sem_send.at[16])
    drain(tokens, sem_send.at[17])
    drain(srecv.at[0:NF - 1], sem_send.at[18])
    drain(nrecv.at[0:NF - 1], sem_send.at[21])

    @pl.when(f > 0)
    def _():
        drain(grecv.at[0], sem_send.at[19])

    @pl.when(f < NF - 1)
    def _():
        drain(grecv.at[1], sem_send.at[20])


def local(enc_q, enc_k, enc_v, enc_cot, cross_k, cross_v, dec_q, dec_cot, frame_lengths):
    G = enc_q.shape[1] // HD
    NF = lax.axis_size("seq") // G
    R = G // 2
    TC = 2 * TB * G
    NW = (G + 2) * FB
    frames = jax.ShapeDtypeStruct(enc_q.shape, BF16)
    tokens = jax.ShapeDtypeStruct(dec_q.shape, BF16)
    any_spec = pl.BlockSpec(memory_space=pl.ANY)
    v = pltpu.VMEM
    scratch = [
        v((G * FB, HD), BF16), v((G * FB, HD), BF16),
        v((2 * G * FB, HD), BF16), v((2 * G * FB, HD), BF16),
        v((HD, 2 * G * FB), BF16), v((HD, 2 * G * FB), BF16),
        v((G * FB, HD), BF16), v((G * FB, HD), BF16),
        v((HD, G * FB), BF16), v((HD, G * FB), BF16),
        v((NF * TC, HD), BF16), v((NF * TC, HD), BF16),
        v((NF, G * FB, TC), BF16),
        v((NW, 2 * FB), F32),
        v((NW, 2 * FB), BF16), v((NW, 2 * FB), BF16),
        v((2 * G * FB, HD), F32),
        v((NF, HD, TC), BF16), v((NF, HD, TC), BF16),
        v((NF, 8, TC), F32), v((NF, 8, TC), F32), v((NF, 8, TC), F32),
        v((NF, HD, TC), BF16), v((NF, HD, TC), BF16),
        v((G * FB, HD), BF16), v((G * FB, HD), BF16),
        v((G * FB, HD), BF16), v((G * FB, HD), BF16),
        v((2 * G * FB, HD), F32), v((2 * G * FB, HD), F32),
        v((G * FB, HD), F32), v((G * FB, HD), F32),
        v((2, 2, R * FB, HD), BF16), v((2, 2, R * FB, HD), BF16),
        v((G * FB, HD), BF16), v((G * FB, HD), BF16),
        v((TC, HD), BF16), v((TC, HD), BF16),
        pltpu.SemaphoreType.DMA((6,)),
        pltpu.SemaphoreType.DMA((2, 2)),
        pltpu.SemaphoreType.DMA((2, NF)),
        pltpu.SemaphoreType.DMA(()),
        pltpu.SemaphoreType.DMA(()),
        pltpu.SemaphoreType.DMA((NF,)),
        pltpu.SemaphoreType.DMA(()),
        pltpu.SemaphoreType.DMA((2,)),
        pltpu.SemaphoreType.DMA((8,)),
        pltpu.SemaphoreType.DMA((26,)),
    ]
    return pl.pallas_call(
        functools.partial(kernel, G, NF),
        out_shape=(frames, frames, frames, frames, tokens, tokens, frames, frames),
        in_specs=[pl.BlockSpec(memory_space=pltpu.SMEM)] + [any_spec] * 8,
        out_specs=(any_spec,) * 8,
        scratch_shapes=scratch,
        compiler_params=pltpu.CompilerParams(
            collective_id=0, has_side_effects=True, vmem_limit_bytes=48 << 20
        ),
    )(frame_lengths, enc_q, enc_k, enc_v, enc_cot, cross_k, cross_v, dec_q, dec_cot)


def solution(mesh):
    frames = P("seq", "grp")
    tokens = P(("seq", "grp"), None)
    return jax.shard_map(
        local,
        mesh=mesh,
        in_specs=(frames,) * 6 + (tokens,) * 2 + (P(),),
        out_specs=(frames,) * 4 + (tokens,) * 2 + (frames,) * 2,
        check_vma=False,
    )
```

profile of v0, /device:TPU:21, one launch (start us, length us, event | category | flops | bytes accessed | tf_op | source)
XLA Modules:
  0.0 99.0 jit_solution(12278071234420781588)
XLA Ops:
  0.6 0.0 copy-start
  0.6 0.9 copy-done
  1.6 0.0 copy-start.1
  1.6 0.9 copy-done.1
  2.5 0.0 copy-start.2
  2.5 0.9 copy-done.2
  3.5 0.0 copy-start.3
  3.5 0.9 copy-done.3
  4.4 0.0 copy-start.4
  4.4 0.9 copy-done.4
  5.4 0.9 copy-done.5
  6.3 0.0 copy-start.6
  6.3 0.8 copy-done.6
  7.2 0.8 copy-done.7
  8.0 0.7 copy-done.8
  8.7 84.8 %shard_map.152 = (bf16[128,1024]{1,0:T(8,128)(2,1)S(1)}, bf16[128,1024]{1,0:T(8,128)(2,1)S(1)}, bf16[128,1024]{1,0:T(8,128)(2,1)S(1)}, bf16[128,1024]{1,0:T(8,12...) custom-call(s32[64]{0:T(128)S(1)} %copy-done.8, ...), custom_call_target="tpu_custom_call" | custom-call | tf_op jit(solution)/shard_map/pallas_call | solution.py:463
  93.5 0.7 copy.25
  94.2 0.7 copy.26
  94.9 0.7 copy.27
  95.6 0.7 copy.28
  96.3 0.6 copy.29
  96.9 0.6 copy.30
  97.6 0.7 copy.31
  98.3 0.7 copy.32
  (3 shorter events, 0.0 us)
Async XLA Ops:
  0.6 1.0 copy-start
  1.6 0.9 copy-start.1
  2.5 0.9 copy-start.2
  3.5 0.9 copy-start.3
  4.4 0.9 copy-start.4
  5.4 0.9 copy-start.5
  6.3 0.8 copy-start.6
  7.2 0.8 copy-start.7
  8.0 0.7 copy-start.8
where the time goes:
time: 99.4 us; the launch traced here: 99 us
  Pallas kernels  84.8 us (85%)
  local copies, waits for them, and re-layouts  13.5 us (14%)
    pallas_call x1, Pallas kernels, local(): pl.pallas_call(functools.partial(kernel, G, NF), out_shape=(frames, frame...  84.8 us
    unnamed x26, local copies, waits for them, and re-layouts  13.5 us

commit v1 on v0

v1 whole, which is shorter than its diff:
```python
import functools
import math

import jax
import jax.numpy as jnp
from jax import lax
from jax.experimental import pallas as pl
from jax.experimental.pallas import tpu as pltpu
from jax.sharding import PartitionSpec as P

HD = 128
FB = 128
TB = 16
SCALE = HD ** (-0.5)
C2 = SCALE * math.log2(math.e)
NEG = -1e30
F32 = jnp.float32
BF16 = jnp.bfloat16
MESH = pl.DeviceIdType.MESH
VMEM_ALL = 67043328


def nt(a, b):
    return lax.dot_general(a, b, (((1,), (1,)), ((), ())), preferred_element_type=F32)


def nn(a, b):
    return lax.dot_general(a, b, (((1,), (0,)), ((), ())), preferred_element_type=F32)


def drain(ref, sem):
    pltpu.make_async_copy(ref, ref, sem).wait()


def lanes(column, width):
    return column if width == HD else jnp.concatenate([column] * (width // HD), axis=1)


def kernel(
    G, NF, len_ref, eq, ek, ev, ec, ckh, cvh, dqh, dch,
    o_eo, o_edq, o_edk, o_edv, o_do, o_ddq, o_cdk, o_cdv,
    eqb, ecb, ekb, evb, ekT, evT, ckb, cvb, ckT, cvT, qt, ct, pbuf, dbuf, sbuf, wbuf, dsbuf,
    bias, nsend, nrecv, ssend, srecv, stat, dqsend, dqrecv,
    eos, edqs, edks, edvs, eka, eva, gsend, grecv, cdks, cdvs, toko, tokdq,
    sem_in, sem_halo, sem_tok, sem_num, sem_st, sem_stat, sem_dq, sem_grad, sem_out, sem_send,
):
    R = G // 2
    TC = 2 * TB * G
    W = 2 * FB
    s = lax.axis_index("seq")
    g = lax.axis_index("grp")
    fo = lax.div(s, G)
    r = lax.rem(s, G)
    x, yl = lax.div(fo, 2), lax.rem(fo, 2)
    z, c = lax.div(r, 2), lax.rem(r, 2)
    f = 2 * x + c
    h = yl * R + z
    same = yl == c
    split = yl != c
    col = pl.ds(pl.multiple_of(h * HD, HD), HD)

    def worker(group, head):
        return (lax.div(group, 2) * 2 + lax.div(head, R)) * G + lax.rem(head, R) * 2 + lax.rem(group, 2)

    def send(src, dst, ssem, rsem, ts, tg):
        pltpu.make_async_remote_copy(
            src_ref=src, dst_ref=dst, send_sem=ssem, recv_sem=rsem,
            device_id=(ts, tg), device_id_type=MESH,
        ).start()

    def move(n, src, dst, ssem, rsem, ts, tg):
        if n > 0:
            send(src, dst, ssem, rsem, ts, tg)
            return

        @pl.when(same)
        def _():
            pltpu.make_async_copy(src, dst, rsem).start()

        @pl.when(split)
        def _():
            send(src, dst, ssem, rsem, ts, tg)

    def cols(ref, head):
        return ref.at[:, pl.ds(pl.multiple_of(head * HD, HD), HD)]

    def rows(ref, index, size):
        return ref.at[pl.ds(pl.multiple_of(index * size, size), size), :]

    barrier = pltpu.get_barrier_semaphore()

    def greet(ts, tg):
        pl.semaphore_signal(barrier, inc=1, device_id=(ts, tg), device_id_type=MESH)

    for n in range(1, NF):
        greet(worker(lax.rem(f + n, NF), h), g)
    for n in range(G):
        greet(worker(fo, lax.rem(h + n, G)), 1 - g)
        greet(f * G + lax.rem(r + n, G), 1 - g)
    for n in range(1, G):
        greet(worker(fo, lax.rem(h + n, G)), g)
        greet(f * G + lax.rem(r + n, G), g)

    @pl.when(split)
    def _():
        greet(worker(fo, h), g)
        greet(f * G + r, g)

    row = lax.broadcasted_iota(jnp.int32, (FB, HD), 0)
    for blk in range(2 * G):
        gb = f * G - R + blk
        length = len_ref[jnp.clip(gb, 0, NF * G - 1)]
        length = jnp.where((gb >= 0) & (gb < NF * G), length, 0)
        bias[blk * FB:(blk + 1) * FB, :] = jnp.where(row < length, 0.0, NEG).astype(F32)
    zero = jnp.zeros((R * FB, HD), BF16)

    @pl.when(f == 0)
    def _():
        ekb[0:R * FB, :] = zero
        evb[0:R * FB, :] = zero

    @pl.when(f == NF - 1)
    def _():
        ekb[(R + G) * FB:, :] = zero
        evb[(R + G) * FB:, :] = zero

    eka[...] = jnp.zeros(eka.shape, F32)
    eva[...] = jnp.zeros(eva.shape, F32)

    pl.semaphore_wait(barrier, 4 * G + NF - 1 - 2 * jnp.where(same, 1, 0))

    place = r * 2 + g
    own_tok = fo * (2 * G) + place
    for n in range(2 * G):
        to = lax.rem(h * 2 + g + n, 2 * G)
        th, tg = lax.div(to, 2), lax.rem(to, 2)
        ts = worker(fo, th)
        move(n, cols(dqh, tg * G + th), rows(qt, own_tok, TB), sem_send.at[0], sem_tok.at[0, fo], ts, tg)
        move(n, cols(dch, tg * G + th), rows(ct, own_tok, TB), sem_send.at[1], sem_tok.at[1, fo], ts, tg)

    def spread(src, dst, slot, ks, ki):
        for n in range(G):
            p = lax.rem(h + n, G)
            move(n, cols(src, p), rows(dst, slot, FB), sem_send.at[ks], sem_in.at[ki], worker(fo, p), g)

    spread(ek, ekb, R + r, 4, 2)
    spread(ev, evb, R + r, 5, 3)

    drain(rows(qt, f, TC), sem_tok.at[0, f])
    for n in range(1, NF):
        to = lax.rem(f + n, NF)
        send(rows(qt, f, TC), rows(qt, f, TC), sem_send.at[10], sem_tok.at[0, f], worker(to, h), g)
    spread(ckh, ckb, r, 2, 0)
    spread(cvh, cvb, r, 3, 1)

    drain(ekb.at[R * FB:(R + G) * FB, :], sem_in.at[2])
    drain(evb.at[R * FB:(R + G) * FB, :], sem_in.at[3])

    @pl.when(f > 0)
    def _():
        for k, ref in enumerate((ekb, evb)):
            send(
                ref.at[R * FB:2 * R * FB, :], ref.at[(R + G) * FB:(2 * R + G) * FB, :],
                sem_send.at[8 + k], sem_halo.at[k, 0], worker(f - 1, h), g,
            )

    @pl.when(f < NF - 1)
    def _():
        for k, ref in enumerate((ekb, evb)):
            send(
                ref.at[G * FB:(R + G) * FB, :], ref.at[0:R * FB, :],
                sem_send.at[26 + k], sem_halo.at[k, 1], worker(f + 1, h), g,
            )

    spread(eq, eqb, r, 6, 4)
    spread(ec, ecb, r, 7, 5)

    row8 = lax.broadcasted_iota(jnp.int32, (8, TC), 0)

    def pack(a, b, c):
        return jnp.where(row8 == 0, a, jnp.where(row8 == 1, b, c))

    drain(ckb, sem_in.at[0])
    drain(cvb, sem_in.at[1])
    drain(rows(ct, f, TC), sem_tok.at[1, f])
    for n in range(1, NF):
        to = lax.rem(f + n, NF)
        send(rows(ct, f, TC), rows(ct, f, TC), sem_send.at[11], sem_tok.at[1, f], worker(to, h), g)
    cvT[...] = cvb[...].T
    ckT[...] = ckb[...].T

    def chunk(t):
        return pl.ds(pl.multiple_of(t * TC, TC), TC)

    def cross_forward(t):
        q = qt[chunk(t), :]
        top = None
        for u in range(G // 2):
            part = nt(ckb[u * W:(u + 1) * W, :], q)
            part = part + lanes(bias[(R * FB) + u * W:(R * FB) + (u + 1) * W, :], TC)
            sbuf[u * W:(u + 1) * W, 0:TC] = part
            high = jnp.max(part, axis=0, keepdims=True)
            top = high if top is None else jnp.maximum(top, high)
        total = jnp.zeros((1, TC), F32)
        for u in range(G // 2):
            expo = jnp.exp2((sbuf[u * W:(u + 1) * W, 0:TC] - top) * C2)
            total = total + jnp.sum(expo, axis=0, keepdims=True)
            pbuf[u * W:(u + 1) * W, chunk(t)] = expo.astype(BF16)
        numer = nn(cvT[...], pbuf[:, chunk(t)])
        nsend[t] = numer.astype(BF16)
        ssend[t] = pack(top, total, total)

    cross_forward(f)
    nrecv[f] = nsend[f]
    srecv[f] = ssend[f]

    @pl.loop(1, NF)
    def _(i):
        t = lax.rem(f + i, NF)
        drain(rows(qt, t, TC), sem_tok.at[0, t])
        cross_forward(t)
        send(nsend.at[t], nrecv.at[f], sem_send.at[12], sem_num, worker(t, h), g)
        send(ssend.at[t], srecv.at[f], sem_send.at[13], sem_st, worker(t, h), g)

    drain(eqb, sem_in.at[4])
    drain(ecb, sem_in.at[5])

    @pl.when(f > 0)
    def _():
        drain(rows(ekb, 0, R * FB), sem_halo.at[0, 1])
        drain(rows(evb, 0, R * FB), sem_halo.at[1, 1])

    @pl.when(f < NF - 1)
    def _():
        drain(rows(ekb, 0, R * FB), sem_halo.at[0, 0])
        drain(rows(evb, 0, R * FB), sem_halo.at[1, 0])

    ekT[...] = ekb[...].T
    evT[...] = evb[...].T

    NU = (G + 2) // 2
    urow = lax.broadcasted_iota(jnp.int32, (W, W), 0)
    ulane = lax.broadcasted_iota(jnp.int32, (W, W), 1)

    def home(src, b, dst, ks, ko):
        away = f * G + b

        @pl.when(away != s)
        def _():
            send(rows(src, b, FB), dst.at[:, col], sem_send.at[ks], sem_out.at[ko], away, g)

        @pl.when(away == s)
        def _():
            pltpu.make_async_copy(rows(src, b, FB), dst.at[:, col], sem_out.at[ko]).start()

    def encoder_pair(j):
        base = pl.multiple_of(j * W, W)
        q = eqb[pl.ds(base, W), :]
        cot = ecb[pl.ds(base, W), :]
        top = None
        for u in range(NU):
            at = pl.multiple_of(base + u * W, W)
            part = nt(ekb[pl.ds(at, W), :], q) + lanes(bias[pl.ds(at, W), :], W)
            if u == 0:
                part = jnp.where((urow < FB) & (ulane >= FB), NEG, part)
            if u == NU - 1:
                part = jnp.where((urow >= FB) & (ulane < FB), NEG, part)
            sbuf[u * W:(u + 1) * W, :] = part
            high = jnp.max(part, axis=0, keepdims=True)
            top = high if top is None else jnp.maximum(top, high)
        total = jnp.zeros((1, W), F32)
        for u in range(NU):
            expo = jnp.exp2((sbuf[u * W:(u + 1) * W, :] - top) * C2)
            total = total + jnp.sum(expo, axis=0, keepdims=True)
            sbuf[u * W:(u + 1) * W, :] = expo
            wbuf[u * W:(u + 1) * W, :] = expo.astype(BF16)
        numer = nn(evT[:, pl.ds(base, NU * W)], wbuf[...])
        out = (numer / total).astype(BF16).astype(F32)
        delta = jnp.sum(cot.astype(F32).T * out, axis=0, keepdims=True)
        eos[pl.ds(base, W), :] = out.T.astype(BF16)
        inv = 1.0 / total
        for u in range(NU):
            at = pl.multiple_of(base + u * W, W)
            prob = sbuf[u * W:(u + 1) * W, :] * inv
            dprob = nt(evb[pl.ds(at, W), :], cot)
            ds = (prob * (dprob - delta)).astype(BF16)
            dsbuf[u * W:(u + 1) * W, :] = ds
            eka[pl.ds(at, W), :] += nn(ds, q)
            eva[pl.ds(at, W), :] += nn(prob.astype(BF16), cot)
        dq = nn(ekT[:, pl.ds(base, NU * W)], dsbuf[...]) * SCALE
        edqs[pl.ds(base, W), :] = dq.T.astype(BF16)
        for half in range(2):
            home(eos, 2 * j + half, o_eo, 14, 0)
            home(edqs, 2 * j + half, o_edq, 15, 1)

    def chunk_home(src, dst, k):
        mine = pl.ds(pl.multiple_of((g * G + h) * HD, HD), HD)
        for n in range(2 * G):
            to = lax.rem(place + n, 2 * G)
            tr, tg = lax.div(to, 2), lax.rem(to, 2)
            move(n, rows(src, to, TB), dst.at[:, mine], sem_send.at[k], sem_out.at[k - 12], f * G + tr, tg)

    def combine():
        drain(nrecv.at[0:NF - 1], sem_num)
        drain(srecv.at[0:NF - 1], sem_st)
        top = srecv[0, 0:1, :]
        for n in range(1, NF):
            top = jnp.maximum(top, srecv[n, 0:1, :])
        total = jnp.zeros((1, TC), F32)
        numer = jnp.zeros((HD, TC), F32)
        for n in range(NF):
            share = jnp.exp2((srecv[n, 0:1, :] - top) * C2)
            total = total + share * srecv[n, 1:2, :]
            numer = numer + share * nrecv[n].astype(F32)
        out = (numer / total).astype(BF16).astype(F32)
        delta = jnp.sum(ct[chunk(f), :].astype(F32).T * out, axis=0, keepdims=True)
        toko[...] = out.T.astype(BF16)
        stat[f] = pack(top, 1.0 / total, delta)
        for n in range(1, NF):
            to = lax.rem(f + n, NF)
            send(stat.at[f], stat.at[f], sem_send.at[18], sem_stat.at[f], worker(to, h), g)
        chunk_home(toko, o_do, 16)

    @pl.loop(0, G // 4)
    def _(j):
        encoder_pair(j)

    @pl.when(f > 0)
    def _():
        gsend[0, 0] = (eka[0:R * FB, :] * SCALE).astype(BF16)
        gsend[0, 1] = eva[0:R * FB, :].astype(BF16)
        send(gsend.at[0], grecv.at[1], sem_send.at[19], sem_grad.at[1], worker(f - 1, h), g)

    combine()

    @pl.loop(G // 4, G // 2)
    def _(j):
        encoder_pair(j)

    @pl.when(f < NF - 1)
    def _():
        gsend[1, 0] = (eka[(R + G) * FB:, :] * SCALE).astype(BF16)
        gsend[1, 1] = eva[(R + G) * FB:, :].astype(BF16)
        send(gsend.at[1], grecv.at[0], sem_send.at[20], sem_grad.at[0], worker(f + 1, h), g)

    def cross_backward(t):
        cot = ct[chunk(t), :]
        share = jnp.exp2((ssend[t, 0:1, :] - stat[t, 0:1, :]) * C2) * stat[t, 1:2, :]
        delta = stat[t, 2:3, :]
        for u in range(G // 2):
            here = slice(u * W, (u + 1) * W)
            prob = pbuf[here, chunk(t)].astype(F32) * share
            dprob = nt(cvb[here, :], cot)
            dbuf[here, chunk(t)] = (prob * (dprob - delta)).astype(BF16)
            pbuf[here, chunk(t)] = prob.astype(BF16)
        dqsend[t] = nn(ckT[...], dbuf[:, chunk(t)]).astype(BF16)

    @pl.loop(1, NF)
    def _(i):
        t = lax.rem(f + i, NF)
        drain(rows(ct, t, TC), sem_tok.at[1, t])
        drain(stat.at[t], sem_stat.at[t])
        cross_backward(t)
        send(dqsend.at[t], dqrecv.at[f], sem_send.at[21], sem_dq, worker(t, h), g)

    cross_backward(f)
    dqrecv[f] = dqsend[f]

    own = slice(R * FB, (R + G) * FB)
    edks[...] = (eka[own, :] * SCALE).astype(BF16)
    edvs[...] = eva[own, :].astype(BF16)

    @pl.when(f > 0)
    def _():
        drain(grecv.at[0], sem_grad.at[0])
        edks[0:R * FB, :] = (eka[R * FB:2 * R * FB, :] * SCALE + grecv[0, 0].astype(F32)).astype(BF16)
        edvs[0:R * FB, :] = (eva[R * FB:2 * R * FB, :] + grecv[0, 1].astype(F32)).astype(BF16)

    @pl.when(f < NF - 1)
    def _():
        drain(grecv.at[1], sem_grad.at[1])
        edks[R * FB:, :] = (eka[2 * R * FB:3 * R * FB, :] * SCALE + grecv[1, 0].astype(F32)).astype(BF16)
        edvs[R * FB:, :] = (eva[2 * R * FB:3 * R * FB, :] + grecv[1, 1].astype(F32)).astype(BF16)

    for n in range(G):
        b = lax.rem(r + n, G)
        home(edks, b, o_edk, 22, 2)
        home(edvs, b, o_edv, 23, 3)

    def cross_grads(n):
        u = lax.rem(z + n, G // 2)
        here = pl.ds(pl.multiple_of(u * W, W), W)
        cdks[here, :] = (nn(dbuf[here, :], qt[...]) * SCALE).astype(BF16)
        cdvs[here, :] = nn(pbuf[here, :], ct[...]).astype(BF16)
        for half in range(2):
            home(cdks, 2 * u + half, o_cdk, 24, 6)
            home(cdvs, 2 * u + half, o_cdv, 25, 7)

    @pl.loop(0, G // 4)
    def _(n):
        cross_grads(n)

    drain(dqrecv.at[0:NF - 1], sem_dq)
    dq = dqrecv[0].astype(F32)
    for n in range(1, NF):
        dq = dq + dqrecv[n].astype(F32)
    tokdq[...] = (dq * SCALE).T.astype(BF16)
    chunk_home(tokdq, o_ddq, 17)

    @pl.loop(G // 4, G // 2)
    def _(n):
        cross_grads(n)

    for k, ref in enumerate((o_eo, o_edq, o_edk, o_edv, o_do, o_ddq, o_cdk, o_cdv)):
        drain(ref, sem_out.at[k])

    def sent(kept):
        for k in (2, 3, 4, 5, 6, 7, 14, 15, 22, 23, 24, 25):
            drain(eqb.at[0:(G - kept) * FB, :], sem_send.at[k])
        for k in (0, 1, 16, 17):
            drain(qt.at[0:(2 * G - kept) * TB, :], sem_send.at[k])

    @pl.when(same)
    def _():
        sent(1)

    @pl.when(split)
    def _():
        sent(0)

    drain(qt.at[0:(NF - 1) * TC, :], sem_send.at[10])
    drain(qt.at[0:(NF - 1) * TC, :], sem_send.at[11])
    drain(nrecv.at[0:NF - 1], sem_send.at[12])
    drain(srecv.at[0:NF - 1], sem_send.at[13])
    drain(srecv.at[0:NF - 1], sem_send.at[18])
    drain(nrecv.at[0:NF - 1], sem_send.at[21])

    @pl.when(f > 0)
    def _():
        drain(rows(ekb, 0, R * FB), sem_send.at[8])
        drain(rows(evb, 0, R * FB), sem_send.at[9])
        drain(grecv.at[0], sem_send.at[19])

    @pl.when(f < NF - 1)
    def _():
        drain(rows(ekb, 0, R * FB), sem_send.at[26])
        drain(rows(evb, 0, R * FB), sem_send.at[27])
        drain(grecv.at[1], sem_send.at[20])


def finish(*refs):
    n = 8
    sources, results, held, sems = refs[:n], refs[n:2 * n], refs[2 * n:3 * n], refs[3 * n]
    for k in range(n):
        pltpu.make_async_copy(sources[k], held[k], sems.at[0, k]).start()
    for k in range(n):
        pltpu.make_async_copy(sources[k], held[k], sems.at[0, k]).wait()
        pltpu.make_async_copy(held[k], results[k], sems.at[1, k]).start()
    for k in range(n):
        pltpu.make_async_copy(held[k], results[k], sems.at[1, k]).wait()


def local(enc_q, enc_k, enc_v, enc_cot, cross_k, cross_v, dec_q, dec_cot, frame_lengths):
    G = enc_q.shape[1] // HD
    NF = lax.axis_size("seq") // G
    R = G // 2
    TC = 2 * TB * G
    NW = (G + 2) * FB
    frames = jax.ShapeDtypeStruct(enc_q.shape, BF16)
    tokens = jax.ShapeDtypeStruct(dec_q.shape, BF16)
    any_spec = pl.BlockSpec(memory_space=pl.ANY)
    v = pltpu.VMEM
    scratch = [
        v((G * FB, HD), BF16), v((G * FB, HD), BF16),
        v((2 * G * FB, HD), BF16), v((2 * G * FB, HD), BF16),
        v((HD, 2 * G * FB), BF16), v((HD, 2 * G * FB), BF16),
        v((G * FB, HD), BF16), v((G * FB, HD), BF16),
        v((HD, G * FB), BF16), v((HD, G * FB), BF16),
        v((NF * TC, HD), BF16), v((NF * TC, HD), BF16),
        v((G * FB, NF * TC), BF16), v((G * FB, NF * TC), BF16),
        v((NW, 2 * FB), F32),
        v((NW, 2 * FB), BF16), v((NW, 2 * FB), BF16),
        v((2 * G * FB, HD), F32),
        v((NF, HD, TC), BF16), v((NF, HD, TC), BF16),
        v((NF, 8, TC), F32), v((NF, 8, TC), F32), v((NF, 8, TC), F32),
        v((NF, HD, TC), BF16), v((NF, HD, TC), BF16),
        v((G * FB, HD), BF16), v((G * FB, HD), BF16),
        v((G * FB, HD), BF16), v((G * FB, HD), BF16),
        v((2 * G * FB, HD), F32), v((2 * G * FB, HD), F32),
        v((2, 2, R * FB, HD), BF16), v((2, 2, R * FB, HD), BF16),
        v((G * FB, HD), BF16), v((G * FB, HD), BF16),
        v((TC, HD), BF16), v((TC, HD), BF16),
        pltpu.SemaphoreType.DMA((6,)),
        pltpu.SemaphoreType.DMA((2, 2)),
        pltpu.SemaphoreType.DMA((2, NF)),
        pltpu.SemaphoreType.DMA(()),
        pltpu.SemaphoreType.DMA(()),
        pltpu.SemaphoreType.DMA((NF,)),
        pltpu.SemaphoreType.DMA(()),
        pltpu.SemaphoreType.DMA((2,)),
        pltpu.SemaphoreType.DMA((8,)),
        pltpu.SemaphoreType.DMA((28,)),
    ]
    shapes = (frames, frames, frames, frames, tokens, tokens, frames, frames)
    staged = pl.pallas_call(
        functools.partial(kernel, G, NF),
        out_shape=shapes,
        in_specs=[pl.BlockSpec(memory_space=pltpu.SMEM)] + [any_spec] * 8,
        out_specs=(any_spec,) * 8,
        scratch_shapes=scratch,
        compiler_params=pltpu.CompilerParams(
            collective_id=0, has_side_effects=True, vmem_limit_bytes=VMEM_ALL
        ),
    )(frame_lengths, enc_q, enc_k, enc_v, enc_cot, cross_k, cross_v, dec_q, dec_cot)
    return pl.pallas_call(
        finish,
        out_shape=shapes,
        in_specs=[any_spec] * 8,
        out_specs=(any_spec,) * 8,
        scratch_shapes=[v(item.shape, BF16) for item in shapes] + [pltpu.SemaphoreType.DMA((2, 8))],
        compiler_params=pltpu.CompilerParams(vmem_limit_bytes=VMEM_ALL),
    )(*staged)


def solution(mesh):
    frames = P("seq", "grp")
    tokens = P(("seq", "grp"), None)
    return jax.shard_map(
        local,
        mesh=mesh,
        in_specs=(frames,) * 6 + (tokens,) * 2 + (P(),),
        out_specs=(frames,) * 4 + (tokens,) * 2 + (frames,) * 2,
        check_vma=False,
    )
```

time: 99.4 us -> 68.3 us (0.69)
  the two profiles are of different devices: /device:TPU:21 before, /device:TPU:1 now
where the time goes in v1:
time: 68.3 us; the launch traced here: 67.7 us
  Pallas kernels  67 us (98%)
    pallas_call x1, Pallas kernels, local(): pl.pallas_call(functools.partial(kernel, G, NF), out_shape=shapes, in_spe...  64.7 us
    pallas_call x1, Pallas kernels, local(): pl.pallas_call(finish, out_shape=shapes, in_specs=[any_spec] * 8, out_spe...  2.27 us

profile of v1, /device:TPU:1, one launch (start us, length us, event | category | flops | bytes accessed | tf_op | source)
XLA Modules:
  0.0 67.7 jit_solution(8467927713214719797)
XLA Ops:
  0.6 64.7 %shard_map.152 = (bf16[128,1024]{1,0:T(8,128)(2,1)}, bf16[128,1024]{1,0:T(8,128)(2,1)}, bf16[128,1024]{1,0:T(8,128)(2,1)}, bf16[128,1024]{1,0:T(8,128)(2,1)}, bf...) custom-call(s32[64]{0:T(128)} %len_ref.1, ...), custom_call_target="tpu_custom_call" | custom-call | tf_op jit(solution)/shard_map/pallas_call | solution.py:505
  65.4 2.3 %shard_map.153 = (bf16[128,1024]{1,0:T(8,128)(2,1)}, bf16[128,1024]{1,0:T(8,128)(2,1)}, bf16[128,1024]{1,0:T(8,128)(2,1)}, bf16[128,1024]{1,0:T(8,128)(2,1)}, bf...) custom-call(bf16[128,1024]{1,0:T(8,128)(2,1)} %get-tuple-element.16.re, ...), custom_call_target="tpu_custom_call" | custom-call | tf_op jit(solution)/shard_map/pallas_call | solution.py:515

commit v2 on v1

--- a/solution.py
+++ b/solution.py
@@ -40,11 +40,12 @@
     G, NF, len_ref, eq, ek, ev, ec, ckh, cvh, dqh, dch,
     o_eo, o_edq, o_edk, o_edv, o_do, o_ddq, o_cdk, o_cdv,
     eqb, ecb, ekb, evb, ekT, evT, ckb, cvb, ckT, cvT, qt, ct, pbuf, dbuf, sbuf, wbuf, dsbuf,
-    bias, nsend, nrecv, ssend, srecv, stat, dqsend, dqrecv,
+    bias, nsend, nrecv, npart, numf, ssend, srecv, spart, mloc, stat, dqsend, dqrecv, dqpart, dqown,
     eos, edqs, edks, edvs, eka, eva, gsend, grecv, cdks, cdvs, toko, tokdq,
-    sem_in, sem_halo, sem_tok, sem_num, sem_st, sem_stat, sem_dq, sem_grad, sem_out, sem_send,
+    sem_in, sem_halo, sem_tok, sem_np, sem_num, sem_st, sem_stat, sem_dq, sem_part, sem_grad, sem_out, sem_send,
 ):
     R = G // 2
+    NX = NF // 2
     TC = 2 * TB * G
     W = 2 * FB
     s = lax.axis_index("seq")
@@ -131,61 +132,48 @@
 
     place = r * 2 + g
     own_tok = fo * (2 * G) + place
-    for n in range(2 * G):
-        to = lax.rem(h * 2 + g + n, 2 * G)
-        th, tg = lax.div(to, 2), lax.rem(to, 2)
-        ts = worker(fo, th)
-        move(n, cols(dqh, tg * G + th), rows(qt, own_tok, TB), sem_send.at[0], sem_tok.at[0, fo], ts, tg)
-        move(n, cols(dch, tg * G + th), rows(ct, own_tok, TB), sem_send.at[1], sem_tok.at[1, fo], ts, tg)
+
+    def tokens_out(src, dst, k):
+        for n in range(2 * G):
+            to = lax.rem(h * 2 + g + n, 2 * G)
+            th, tg = lax.div(to, 2), lax.rem(to, 2)
+            move(n, cols(src, tg * G + th), rows(dst, own_tok, TB), sem_send.at[k], sem_tok.at[k, fo], worker(fo, th), tg)
+
+    tokens_out(dqh, qt, 0)
 
     def spread(src, dst, slot, ks, ki):
         for n in range(G):
             p = lax.rem(h + n, G)
             move(n, cols(src, p), rows(dst, slot, FB), sem_send.at[ks], sem_in.at[ki], worker(fo, p), g)
 
+    spread(ckh, ckb, r, 2, 0)
+    spread(cvh, cvb, r, 3, 1)
+
+    drain(rows(qt, f, TC), sem_tok.at[0, f])
+    partner = worker(2 * x + 1 - c, h)
+
+    def same_core(i):
+        return 2 * lax.rem(x + i, NX) + c
+
+    def other_core(i):
+        return 2 * lax.rem(x + i, NX) + 1 - c
+
+    for n in range(1, NX):
+        send(rows(qt, f, TC), rows(qt, f, TC), sem_send.at[10], sem_tok.at[0, f], worker(same_core(n), h), g)
+    send(rows(qt, f, TC), rows(qt, f, TC), sem_send.at[29], sem_tok.at[0, f], partner, g)
     spread(ek, ekb, R + r, 4, 2)
     spread(ev, evb, R + r, 5, 3)
 
-    drain(rows(qt, f, TC), sem_tok.at[0, f])
-    for n in range(1, NF):
-        to = lax.rem(f + n, NF)
-        send(rows(qt, f, TC), rows(qt, f, TC), sem_send.at[10], sem_tok.at[0, f], worker(to, h), g)
-    spread(ckh, ckb, r, 2, 0)
-    spread(cvh, cvb, r, 3, 1)
-
-    drain(ekb.at[R * FB:(R + G) * FB, :], sem_in.at[2])
-    drain(evb.at[R * FB:(R + G) * FB, :], sem_in.at[3])
-
-    @pl.when(f > 0)
-    def _():
-        for k, ref in enumerate((ekb, evb)):
-            send(
-                ref.at[R * FB:2 * R * FB, :], ref.at[(R + G) * FB:(2 * R + G) * FB, :],
-                sem_send.at[8 + k], sem_halo.at[k, 0], worker(f - 1, h), g,
-            )
-
-    @pl.when(f < NF - 1)
-    def _():
-        for k, ref in enumerate((ekb, evb)):
-            send(
-                ref.at[G * FB:(R + G) * FB, :], ref.at[0:R * FB, :],
-                sem_send.at[26 + k], sem_halo.at[k, 1], worker(f + 1, h), g,
-            )
-
+    row8 = lax.broadcasted_iota(jnp.int32, (8, TC), 0)
+
+    def pack(a, b, c):
+        return jnp.where(row8 == 0, a, jnp.where(row8 == 1, b, c))
+
+    drain(ckb, sem_in.at[0])
+    drain(cvb, sem_in.at[1])
     spread(eq, eqb, r, 6, 4)
     spread(ec, ecb, r, 7, 5)
-
-    row8 = lax.broadcasted_iota(jnp.int32, (8, TC), 0)
-
-    def pack(a, b, c):
-        return jnp.where(row8 == 0, a, jnp.where(row8 == 1, b, c))
-
-    drain(ckb, sem_in.at[0])
-    drain(cvb, sem_in.at[1])
-    drain(rows(ct, f, TC), sem_tok.at[1, f])
-    for n in range(1, NF):
-        to = lax.rem(f + n, NF)
-        send(rows(ct, f, TC), rows(ct, f, TC), sem_send.at[11], sem_tok.at[1, f], worker(to, h), g)
+    tokens_out(dch, ct, 1)
     cvT[...] = cvb[...].T
     ckT[...] = ckb[...].T
 
@@ -206,21 +194,74 @@
             expo = jnp.exp2((sbuf[u * W:(u + 1) * W, 0:TC] - top) * C2)
             total = total + jnp.sum(expo, axis=0, keepdims=True)
             pbuf[u * W:(u + 1) * W, chunk(t)] = expo.astype(BF16)
-        numer = nn(cvT[...], pbuf[:, chunk(t)])
-        nsend[t] = numer.astype(BF16)
-        ssend[t] = pack(top, total, total)
-
-    cross_forward(f)
-    nrecv[f] = nsend[f]
-    srecv[f] = ssend[f]
-
-    @pl.loop(1, NF)
-    def _(i):
-        t = lax.rem(f + i, NF)
+        mloc[t] = pack(top, total, total)
+        return nn(cvT[...], pbuf[:, chunk(t)])
+
+    numf[x] = cross_forward(f)
+
+    def halo_out(k, ref):
+        drain(ref.at[R * FB:(R + G) * FB, :], sem_in.at[2 + k])
+
+        @pl.when(f > 0)
+        def _():
+            send(
+                ref.at[R * FB:2 * R * FB, :], ref.at[(R + G) * FB:(2 * R + G) * FB, :],
+                sem_send.at[8 + k], sem_halo.at[k, 0], worker(f - 1, h), g,
+            )
+
+        @pl.when(f < NF - 1)
+        def _():
+            send(
+                ref.at[G * FB:(R + G) * FB, :], ref.at[0:R * FB, :],
+                sem_send.at[26 + k], sem_halo.at[k, 1], worker(f + 1, h), g,
+            )
+
+    @pl.loop(1, NX)
+    def _(i):
+        t = same_core(i)
         drain(rows(qt, t, TC), sem_tok.at[0, t])
-        cross_forward(t)
-        send(nsend.at[t], nrecv.at[f], sem_send.at[12], sem_num, worker(t, h), g)
-        send(ssend.at[t], srecv.at[f], sem_send.at[13], sem_st, worker(t, h), g)
+        send(rows(qt, t, TC), rows(qt, t, TC), sem_send.at[29], sem_tok.at[0, t], partner, g)
+        numf[lax.rem(x + i, NX)] = cross_forward(t)
+
+    halo_out(0, ekb)
+
+    def for_partner(i):
+        t = other_core(i)
+        drain(rows(qt, t, TC), sem_tok.at[0, t])
+        nsend[t] = cross_forward(t).astype(BF16)
+        send(nsend.at[t], npart.at[t], sem_send.at[30], sem_np.at[0, t], partner, g)
+        send(mloc.at[t], spart.at[t], sem_send.at[31], sem_np.at[1, t], partner, g)
+
+    @pl.loop(0, NX // 2)
+    def _(i):
+        for_partner(i)
+
+    halo_out(1, evb)
+
+    @pl.loop(NX // 2, NX)
+    def _(i):
+        for_partner(i)
+
+    def joined(i):
+        t = same_core(i)
+        drain(npart.at[t], sem_np.at[0, t])
+        drain(spart.at[t], sem_np.at[1, t])
+        top = jnp.maximum(mloc[t, 0:1, :], spart[t, 0:1, :])
+        mine = jnp.exp2((mloc[t, 0:1, :] - top) * C2)
+        theirs = jnp.exp2((spart[t, 0:1, :] - top) * C2)
+        total = mine * mloc[t, 1:2, :] + theirs * spart[t, 1:2, :]
+        numer = mine * numf[lax.rem(x + i, NX)] + theirs * npart[t].astype(F32)
+        return t, numer.astype(BF16), pack(top, total, total)
+
+    @pl.loop(1, NX)
+    def _(i):
+        t, numer, stats = joined(i)
+        nsend[t] = numer
+        ssend[t] = stats
+        send(nsend.at[t], nrecv.at[x], sem_send.at[12], sem_num, worker(t, h), g)
+        send(ssend.at[t], srecv.at[x], sem_send.at[13], sem_st, worker(t, h), g)
+
+    _, nrecv[x], srecv[x] = joined(0)
 
     drain(eqb, sem_in.at[4])
     drain(ecb, sem_in.at[5])
@@ -235,6 +276,10 @@
         drain(rows(ekb, 0, R * FB), sem_halo.at[0, 0])
         drain(rows(evb, 0, R * FB), sem_halo.at[1, 0])
 
+    drain(rows(ct, f, TC), sem_tok.at[1, f])
+    for n in range(1, NF):
+        to = lax.rem(f + n, NF)
+        send(rows(ct, f, TC), rows(ct, f, TC), sem_send.at[11], sem_tok.at[1, f], worker(to, h), g)
     ekT[...] = ekb[...].T
     evT[...] = evb[...].T
 
@@ -301,14 +346,14 @@
             move(n, rows(src, to, TB), dst.at[:, mine], sem_send.at[k], sem_out.at[k - 12], f * G + tr, tg)
 
     def combine():
-        drain(nrecv.at[0:NF - 1], sem_num)
-        drain(srecv.at[0:NF - 1], sem_st)
+        drain(nrecv.at[0:NX - 1], sem_num)
+        drain(srecv.at[0:NX - 1], sem_st)
         top = srecv[0, 0:1, :]
-        for n in range(1, NF):
+        for n in range(1, NX):
             top = jnp.maximum(top, srecv[n, 0:1, :])
         total = jnp.zeros((1, TC), F32)
         numer = jnp.zeros((HD, TC), F32)
-        for n in range(NF):
+        for n in range(NX):
             share = jnp.exp2((srecv[n, 0:1, :] - top) * C2)
             total = total + share * srecv[n, 1:2, :]
             numer = numer + share * nrecv[n].astype(F32)
@@ -321,31 +366,60 @@
             send(stat.at[f], stat.at[f], sem_send.at[18], sem_stat.at[f], worker(to, h), g)
         chunk_home(toko, o_do, 16)
 
+    back = lax.rem(z, 2)
+
+    def pair_at(i):
+        encoder_pair(i * (1 - back) + (G // 2 - 1 - i) * back)
+
+    def rim(side):
+        to = f - 1 + 2 * side
+
+        @pl.when((to >= 0) & (to < NF))
+        def _():
+            edge = pl.ds(pl.multiple_of(side * ((R + G) * FB), R * FB), R * FB)
+            gsend[side, 0] = (eka[edge, :] * SCALE).astype(BF16)
+            gsend[side, 1] = eva[edge, :].astype(BF16)
+            send(gsend.at[side], grecv.at[1 - side], sem_send.at[19 + side], sem_grad.at[1 - side], worker(to, h), g)
+
+    def half_home(half):
+        near = f - 1 + 2 * half
+        into = pl.ds(pl.multiple_of(half * (R * FB), R * FB), R * FB)
+        start = pl.ds(pl.multiple_of((1 + half) * (R * FB), R * FB), R * FB)
+        there = (near >= 0) & (near < NF)
+
+        @pl.when(there)
+        def _():
+            drain(grecv.at[half], sem_grad.at[half])
+            edks[into, :] = (eka[start, :] * SCALE + grecv[half, 0].astype(F32)).astype(BF16)
+            edvs[into, :] = (eva[start, :] + grecv[half, 1].astype(F32)).astype(BF16)
+
+        @pl.when(jnp.logical_not(there))
+        def _():
+            edks[into, :] = (eka[start, :] * SCALE).astype(BF16)
+            edvs[into, :] = eva[start, :].astype(BF16)
+
+        for n in range(R):
+            b = half * R + lax.rem(r + n, R)
+            home(edks, b, o_edk, 22, 2)
+            home(edvs, b, o_edv, 23, 3)
+
     @pl.loop(0, G // 4)
-    def _(j):
-        encoder_pair(j)
-
-    @pl.when(f > 0)
-    def _():
-        gsend[0, 0] = (eka[0:R * FB, :] * SCALE).astype(BF16)
-        gsend[0, 1] = eva[0:R * FB, :].astype(BF16)
-        send(gsend.at[0], grecv.at[1], sem_send.at[19], sem_grad.at[1], worker(f - 1, h), g)
-
+    def _(i):
+        pair_at(i)
+
+    rim(back)
     combine()
 
     @pl.loop(G // 4, G // 2)
-    def _(j):
-        encoder_pair(j)
-
-    @pl.when(f < NF - 1)
-    def _():
-        gsend[1, 0] = (eka[(R + G) * FB:, :] * SCALE).astype(BF16)
-        gsend[1, 1] = eva[(R + G) * FB:, :].astype(BF16)
-        send(gsend.at[1], grecv.at[0], sem_send.at[20], sem_grad.at[0], worker(f + 1, h), g)
+    def _(i):
+        pair_at(i)
+
+    rim(1 - back)
+    half_home(1 - back)
 
     def cross_backward(t):
         cot = ct[chunk(t), :]
-        share = jnp.exp2((ssend[t, 0:1, :] - stat[t, 0:1, :]) * C2) * stat[t, 1:2, :]
+        share = jnp.exp2((mloc[t, 0:1, :] - stat[t, 0:1, :]) * C2) * stat[t, 1:2, :]
         delta = stat[t, 2:3, :]
         for u in range(G // 2):
             here = slice(u * W, (u + 1) * W)
@@ -353,39 +427,29 @@
             dprob = nt(cvb[here, :], cot)
             dbuf[here, chunk(t)] = (prob * (dprob - delta)).astype(BF16)
             pbuf[here, chunk(t)] = prob.astype(BF16)
-        dqsend[t] = nn(ckT[...], dbuf[:, chunk(t)]).astype(BF16)
-
-    @pl.loop(1, NF)
-    def _(i):
-        t = lax.rem(f + i, NF)
+        return nn(ckT[...], dbuf[:, chunk(t)])
+
+    def backward_step(t):
         drain(rows(ct, t, TC), sem_tok.at[1, t])
         drain(stat.at[t], sem_stat.at[t])
-        cross_backward(t)
-        send(dqsend.at[t], dqrecv.at[f], sem_send.at[21], sem_dq, worker(t, h), g)
-
-    cross_backward(f)
-    dqrecv[f] = dqsend[f]
-
-    own = slice(R * FB, (R + G) * FB)
-    edks[...] = (eka[own, :] * SCALE).astype(BF16)
-    edvs[...] = eva[own, :].astype(BF16)
-
-    @pl.when(f > 0)
-    def _():
-        drain(grecv.at[0], sem_grad.at[0])
-        edks[0:R * FB, :] = (eka[R * FB:2 * R * FB, :] * SCALE + grecv[0, 0].astype(F32)).astype(BF16)
-        edvs[0:R * FB, :] = (eva[R * FB:2 * R * FB, :] + grecv[0, 1].astype(F32)).astype(BF16)
-
-    @pl.when(f < NF - 1)
-    def _():
-        drain(grecv.at[1], sem_grad.at[1])
-        edks[R * FB:, :] = (eka[2 * R * FB:3 * R * FB, :] * SCALE + grecv[1, 0].astype(F32)).astype(BF16)
-        edvs[R * FB:, :] = (eva[2 * R * FB:3 * R * FB, :] + grecv[1, 1].astype(F32)).astype(BF16)
-
-    for n in range(G):
-        b = lax.rem(r + n, G)
-        home(edks, b, o_edk, 22, 2)
-        home(edvs, b, o_edv, 23, 3)
+        return cross_backward(t)
+
+    @pl.loop(0, NX)
+    def _(i):
+        t = other_core(i)
+        dqsend[t] = backward_step(t).astype(BF16)
+        send(dqsend.at[t], dqpart.at[t], sem_send.at[28], sem_part.at[t], partner, g)
+
+    @pl.loop(1, NX)
+    def _(i):
+        t = same_core(i)
+        dq = backward_step(t)
+        drain(dqpart.at[t], sem_part.at[t])
+        dqsend[t] = (dq + dqpart[t].astype(F32)).astype(BF16)
+        send(dqsend.at[t], dqrecv.at[x], sem_send.at[21], sem_dq, worker(t, h), g)
+
+    half_home(back)
+    dqown[...] = cross_backward(f)
 
     def cross_grads(n):
         u = lax.rem(z + n, G // 2)
@@ -400,10 +464,11 @@
     def _(n):
         cross_grads(n)
 
-    drain(dqrecv.at[0:NF - 1], sem_dq)
-    dq = dqrecv[0].astype(F32)
-    for n in range(1, NF):
-        dq = dq + dqrecv[n].astype(F32)
+    drain(dqpart.at[f], sem_part.at[f])
+    drain(dqrecv.at[0:NX - 1], sem_dq)
+    dq = dqown[...] + dqpart[f].astype(F32)
+    for n in range(1, NX):
+        dq = dq + dqrecv[lax.rem(x + n, NX)].astype(F32)
     tokdq[...] = (dq * SCALE).T.astype(BF16)
     chunk_home(tokdq, o_ddq, 17)
 
@@ -428,12 +493,16 @@
     def _():
         sent(0)
 
-    drain(qt.at[0:(NF - 1) * TC, :], sem_send.at[10])
+    drain(qt.at[0:(NX - 1) * TC, :], sem_send.at[10])
+    drain(qt.at[0:NX * TC, :], sem_send.at[29])
+    drain(nsend.at[0:NX], sem_send.at[30])
+    drain(stat.at[0:NX], sem_send.at[31])
     drain(qt.at[0:(NF - 1) * TC, :], sem_send.at[11])
-    drain(nrecv.at[0:NF - 1], sem_send.at[12])
-    drain(srecv.at[0:NF - 1], sem_send.at[13])
-    drain(srecv.at[0:NF - 1], sem_send.at[18])
-    drain(nrecv.at[0:NF - 1], sem_send.at[21])
+    drain(nsend.at[0:NX - 1], sem_send.at[12])
+    drain(stat.at[0:NX - 1], sem_send.at[13])
+    drain(stat.at[0:NF - 1], sem_send.at[18])
+    drain(dqrecv.at[0:NX - 1], sem_send.at[21])
+    drain(dqrecv.at[0:NX], sem_send.at[28])
 
     @pl.when(f > 0)
     def _():
@@ -464,6 +533,7 @@
     G = enc_q.shape[1] // HD
     NF = lax.axis_size("seq") // G
     R = G // 2
+    NX = NF // 2
     TC = 2 * TB * G
     NW = (G + 2) * FB
     frames = jax.ShapeDtypeStruct(enc_q.shape, BF16)
@@ -481,9 +551,12 @@
         v((NW, 2 * FB), F32),
         v((NW, 2 * FB), BF16), v((NW, 2 * FB), BF16),
         v((2 * G * FB, HD), F32),
-        v((NF, HD, TC), BF16), v((NF, HD, TC), BF16),
-        v((NF, 8, TC), F32), v((NF, 8, TC), F32), v((NF, 8, TC), F32),
-        v((NF, HD, TC), BF16), v((NF, HD, TC), BF16),
+        v((NF, HD, TC), BF16), v((NX, HD, TC), BF16),
+        v((NF, HD, TC), BF16), v((NX, HD, TC), F32),
+        v((NF, 8, TC), F32), v((NX, 8, TC), F32), v((NF, 8, TC), F32),
+        v((NF, 8, TC), F32), v((NF, 8, TC), F32),
+        v((NF, HD, TC), BF16), v((NX, HD, TC), BF16),
+        v((NF, HD, TC), BF16), v((HD, TC), F32),
         v((G * FB, HD), BF16), v((G * FB, HD), BF16),
         v((G * FB, HD), BF16), v((G * FB, HD), BF16),
         v((2 * G * FB, HD), F32), v((2 * G * FB, HD), F32),
@@ -493,13 +566,15 @@
         pltpu.SemaphoreType.DMA((6,)),
         pltpu.SemaphoreType.DMA((2, 2)),
         pltpu.SemaphoreType.DMA((2, NF)),
+        pltpu.SemaphoreType.DMA((2, NF)),
         pltpu.SemaphoreType.DMA(()),
         pltpu.SemaphoreType.DMA(()),
         pltpu.SemaphoreType.DMA((NF,)),
         pltpu.SemaphoreType.DMA(()),
+        pltpu.SemaphoreType.DMA((NF,)),
         pltpu.SemaphoreType.DMA((2,)),
         pltpu.SemaphoreType.DMA((8,)),
-        pltpu.SemaphoreType.DMA((28,)),
+        pltpu.SemaphoreType.DMA((32,)),
     ]
     shapes = (frames, frames, frames, frames, tokens, tokens, frames, frames)
     staged = pl.pallas_call(

time: 68.3 us -> 63.4 us (0.928)
  Pallas kernels: 67 us -> 62.6 us
    pallas_call x1, Pallas kernels: 64.7 us -> 60.3 us  [local(): pl.pallas_call(functools.partial(kernel, G, NF), out_shape=shapes, in_spe...]
where the time goes in v2:
time: 63.4 us; the launch traced here: 63.2 us
  Pallas kernels  62.6 us (99%)
  between operations  0.64 us (1%)
    pallas_call x1, Pallas kernels, local(): pl.pallas_call(functools.partial(kernel, G, NF), out_shape=shapes, in_spe...  60.3 us
    pallas_call x1, Pallas kernels, local(): pl.pallas_call(finish, out_shape=shapes, in_specs=[any_spec] * 8, out_spe...  2.27 us

profile of v2, /device:TPU:1, one launch (start us, length us, event | category | flops | bytes accessed | tf_op | source)
XLA Modules:
  0.0 63.2 jit_solution(6709349171402944347)
XLA Ops:
  0.6 60.3 %shard_map.152 = (bf16[128,1024]{1,0:T(8,128)(2,1)}, bf16[128,1024]{1,0:T(8,128)(2,1)}, bf16[128,1024]{1,0:T(8,128)(2,1)}, bf16[128,1024]{1,0:T(8,128)(2,1)}, bf...) custom-call(s32[64]{0:T(128)} %len_ref.1, ...), custom_call_target="tpu_custom_call" | custom-call | tf_op jit(solution)/shard_map/pallas_call | solution.py:580
  60.9 2.3 %shard_map.153 = (bf16[128,1024]{1,0:T(8,128)(2,1)}, bf16[128,1024]{1,0:T(8,128)(2,1)}, bf16[128,1024]{1,0:T(8,128)(2,1)}, bf16[128,1024]{1,0:T(8,128)(2,1)}, bf...) custom-call(bf16[128,1024]{1,0:T(8,128)(2,1)} %get-tuple-element.16.re, ...), custom_call_target="tpu_custom_call" | custom-call | tf_op jit(solution)/shard_map/pallas_call | solution.py:590

commit v3 on v2

--- a/solution.py
+++ b/solution.py
@@ -39,7 +39,7 @@
 def kernel(
     G, NF, len_ref, eq, ek, ev, ec, ckh, cvh, dqh, dch,
     o_eo, o_edq, o_edk, o_edv, o_do, o_ddq, o_cdk, o_cdv,
-    eqb, ecb, ekb, evb, ekT, evT, ckb, cvb, ckT, cvT, qt, ct, pbuf, dbuf, sbuf, wbuf, dsbuf,
+    eqb, ecb, ekb, evb, ekT, evT, ckb, cvb, ckT, cvT, qt, ct, pbuf, dbuf, sbuf, sbuf2, wbuf, wbuf2, dsbuf,
     bias, nsend, nrecv, npart, numf, ssend, srecv, spart, mloc, stat, dqsend, dqrecv, dqpart, dqown,
     eos, edqs, edks, edvs, eka, eva, gsend, grecv, cdks, cdvs, toko, tokdq,
     sem_in, sem_halo, sem_tok, sem_np, sem_num, sem_st, sem_stat, sem_dq, sem_part, sem_grad, sem_out, sem_send,
@@ -224,7 +224,6 @@
         numf[lax.rem(x + i, NX)] = cross_forward(t)
 
     halo_out(0, ekb)
-
     def for_partner(i):
         t = other_core(i)
         drain(rows(qt, t, TC), sem_tok.at[0, t])
@@ -263,25 +262,18 @@
 
     _, nrecv[x], srecv[x] = joined(0)
 
+    def halo_in(k, ref):
+        @pl.when(f > 0)
+        def _():
+            drain(rows(ref, 0, R * FB), sem_halo.at[k, 1])
+
+        @pl.when(f < NF - 1)
+        def _():
+            drain(rows(ref, 0, R * FB), sem_halo.at[k, 0])
+
     drain(eqb, sem_in.at[4])
-    drain(ecb, sem_in.at[5])
-
-    @pl.when(f > 0)
-    def _():
-        drain(rows(ekb, 0, R * FB), sem_halo.at[0, 1])
-        drain(rows(evb, 0, R * FB), sem_halo.at[1, 1])
-
-    @pl.when(f < NF - 1)
-    def _():
-        drain(rows(ekb, 0, R * FB), sem_halo.at[0, 0])
-        drain(rows(evb, 0, R * FB), sem_halo.at[1, 0])
-
-    drain(rows(ct, f, TC), sem_tok.at[1, f])
-    for n in range(1, NF):
-        to = lax.rem(f + n, NF)
-        send(rows(ct, f, TC), rows(ct, f, TC), sem_send.at[11], sem_tok.at[1, f], worker(to, h), g)
+    halo_in(0, ekb)
     ekT[...] = ekb[...].T
-    evT[...] = evb[...].T
 
     NU = (G + 2) // 2
     urow = lax.broadcasted_iota(jnp.int32, (W, W), 0)
@@ -298,45 +290,64 @@
         def _():
             pltpu.make_async_copy(rows(src, b, FB), dst.at[:, col], sem_out.at[ko]).start()
 
-    def encoder_pair(j):
+    def score(j, u, sb):
+        at = pl.ds(pl.multiple_of(j * W + u * W, W), W)
+        q = eqb[pl.ds(pl.multiple_of(j * W, W), W), :]
+        part = nt(ekb[at, :], q) + lanes(bias[at, :], W)
+        if u == 0:
+            part = jnp.where((urow < FB) & (ulane >= FB), NEG, part)
+        if u == NU - 1:
+            part = jnp.where((urow >= FB) & (ulane < FB), NEG, part)
+        sb[u * W:(u + 1) * W, :] = part
+        return jnp.max(part, axis=0, keepdims=True)
+
+    def exponents(top, sb, wb):
+        total = jnp.zeros((1, W), F32)
+        for u in range(NU):
+            expo = jnp.exp2((sb[u * W:(u + 1) * W, :] - top) * C2)
+            total = total + jnp.sum(expo, axis=0, keepdims=True)
+            sb[u * W:(u + 1) * W, :] = expo
+            wb[u * W:(u + 1) * W, :] = expo.astype(BF16)
+        return total
+
+    def output(j, total, wb):
         base = pl.multiple_of(j * W, W)
+        numer = nn(evT[:, pl.ds(base, NU * W)], wb[...])
+        out = (numer / total).astype(BF16).astype(F32)
+        delta = jnp.sum(ecb[pl.ds(base, W), :].astype(F32).T * out, axis=0, keepdims=True)
+        eos[pl.ds(base, W), :] = out.T.astype(BF16)
+        return 1.0 / total, delta
+
+    def gradients(j, u, sb, inv, delta):
+        base = pl.multiple_of(j * W, W)
+        at = pl.multiple_of(base + u * W, W)
         q = eqb[pl.ds(base, W), :]
         cot = ecb[pl.ds(base, W), :]
+        prob = sb[u * W:(u + 1) * W, :] * inv
+        dprob = nt(evb[pl.ds(at, W), :], cot)
+        ds = (prob * (dprob - delta)).astype(BF16)
+        dsbuf[u * W:(u + 1) * W, :] = ds
+        eka[pl.ds(at, W), :] += nn(ds, q)
+        eva[pl.ds(at, W), :] += nn(prob.astype(BF16), cot)
+
+    def pair_step(j, sb, wb, inv, delta, nj, nsb, nwb):
+        base = pl.multiple_of(j * W, W)
         top = None
         for u in range(NU):
-            at = pl.multiple_of(base + u * W, W)
-            part = nt(ekb[pl.ds(at, W), :], q) + lanes(bias[pl.ds(at, W), :], W)
-            if u == 0:
-                part = jnp.where((urow < FB) & (ulane >= FB), NEG, part)
-            if u == NU - 1:
-                part = jnp.where((urow >= FB) & (ulane < FB), NEG, part)
-            sbuf[u * W:(u + 1) * W, :] = part
-            high = jnp.max(part, axis=0, keepdims=True)
-            top = high if top is None else jnp.maximum(top, high)
-        total = jnp.zeros((1, W), F32)
-        for u in range(NU):
-            expo = jnp.exp2((sbuf[u * W:(u + 1) * W, :] - top) * C2)
-            total = total + jnp.sum(expo, axis=0, keepdims=True)
-            sbuf[u * W:(u + 1) * W, :] = expo
-            wbuf[u * W:(u + 1) * W, :] = expo.astype(BF16)
-        numer = nn(evT[:, pl.ds(base, NU * W)], wbuf[...])
-        out = (numer / total).astype(BF16).astype(F32)
-        delta = jnp.sum(cot.astype(F32).T * out, axis=0, keepdims=True)
-        eos[pl.ds(base, W), :] = out.T.astype(BF16)
-        inv = 1.0 / total
-        for u in range(NU):
-            at = pl.multiple_of(base + u * W, W)
-            prob = sbuf[u * W:(u + 1) * W, :] * inv
-            dprob = nt(evb[pl.ds(at, W), :], cot)
-            ds = (prob * (dprob - delta)).astype(BF16)
-            dsbuf[u * W:(u + 1) * W, :] = ds
-            eka[pl.ds(at, W), :] += nn(ds, q)
-            eva[pl.ds(at, W), :] += nn(prob.astype(BF16), cot)
+            gradients(j, u, sb, inv, delta)
+            if nj is not None:
+                high = score(nj, u, nsb)
+                top = high if top is None else jnp.maximum(top, high)
         dq = nn(ekT[:, pl.ds(base, NU * W)], dsbuf[...]) * SCALE
         edqs[pl.ds(base, W), :] = dq.T.astype(BF16)
+        ahead = None
+        if nj is not None:
+            total = exponents(top, nsb, nwb)
+            ahead = output(nj, total, nwb)
         for half in range(2):
             home(eos, 2 * j + half, o_eo, 14, 0)
             home(edqs, 2 * j + half, o_edq, 15, 1)
+        return ahead
 
     def chunk_home(src, dst, k):
         mine = pl.ds(pl.multiple_of((g * G + h) * HD, HD), HD)
@@ -369,7 +380,7 @@
     back = lax.rem(z, 2)
 
     def pair_at(i):
-        encoder_pair(i * (1 - back) + (G // 2 - 1 - i) * back)
+        return i * (1 - back) + (G // 2 - 1 - i) * back
 
     def rim(side):
         to = f - 1 + 2 * side
@@ -403,19 +414,36 @@
             home(edks, b, o_edk, 22, 2)
             home(edvs, b, o_edv, 23, 3)
 
-    @pl.loop(0, G // 4)
-    def _(i):
-        pair_at(i)
-
-    rim(back)
-    combine()
-
-    @pl.loop(G // 4, G // 2)
-    def _(i):
-        pair_at(i)
+    slots = ((sbuf, wbuf), (sbuf2, wbuf2))
+    top = None
+    for u in range(NU):
+        high = score(pair_at(0), u, sbuf)
+        top = high if top is None else jnp.maximum(top, high)
+    total = exponents(top, sbuf, wbuf)
+    halo_in(1, evb)
+    evT[...] = evb[...].T
+    drain(ecb, sem_in.at[5])
+    drain(rows(ct, f, TC), sem_tok.at[1, f])
+    for n in range(1, NX):
+        send(rows(ct, f, TC), rows(ct, f, TC), sem_send.at[11], sem_tok.at[1, f], worker(same_core(n), h), g)
+    send(rows(ct, f, TC), rows(ct, f, TC), sem_send.at[32], sem_tok.at[1, f], partner, g)
+    ahead = output(pair_at(0), total, wbuf)
+    for i in range(G // 2):
+        if i == G // 4:
+            combine()
+            rim(back)
+        if i == G // 2 - 1:
+            for n in range(1, NX):
+                t = same_core(n)
+                drain(rows(ct, t, TC), sem_tok.at[1, t])
+                send(rows(ct, t, TC), rows(ct, t, TC), sem_send.at[32], sem_tok.at[1, t], partner, g)
+        more = i + 1 < G // 2
+        ahead = pair_step(
+            pair_at(i), *slots[i % 2], *ahead,
+            pair_at(i + 1) if more else None, *slots[(i + 1) % 2],
+        )
 
     rim(1 - back)
-    half_home(1 - back)
 
     def cross_backward(t):
         cot = ct[chunk(t), :]
@@ -430,26 +458,32 @@
         return nn(ckT[...], dbuf[:, chunk(t)])
 
     def backward_step(t):
-        drain(rows(ct, t, TC), sem_tok.at[1, t])
         drain(stat.at[t], sem_stat.at[t])
         return cross_backward(t)
 
     @pl.loop(0, NX)
     def _(i):
         t = other_core(i)
+        drain(rows(ct, t, TC), sem_tok.at[1, t])
         dqsend[t] = backward_step(t).astype(BF16)
         send(dqsend.at[t], dqpart.at[t], sem_send.at[28], sem_part.at[t], partner, g)
 
-    @pl.loop(1, NX)
-    def _(i):
+    def for_others(i):
         t = same_core(i)
         dq = backward_step(t)
         drain(dqpart.at[t], sem_part.at[t])
         dqsend[t] = (dq + dqpart[t].astype(F32)).astype(BF16)
         send(dqsend.at[t], dqrecv.at[x], sem_send.at[21], sem_dq, worker(t, h), g)
 
+    half_home(1 - back)
+    dqown[...] = cross_backward(f)
+
+    @pl.loop(1, NX - 1)
+    def _(i):
+        for_others(i)
+
     half_home(back)
-    dqown[...] = cross_backward(f)
+    for_others(NX - 1)
 
     def cross_grads(n):
         u = lax.rem(z + n, G // 2)
@@ -460,7 +494,7 @@
             home(cdks, 2 * u + half, o_cdk, 24, 6)
             home(cdvs, 2 * u + half, o_cdv, 25, 7)
 
-    @pl.loop(0, G // 4)
+    @pl.loop(0, G // 2)
     def _(n):
         cross_grads(n)
 
@@ -472,10 +506,6 @@
     tokdq[...] = (dq * SCALE).T.astype(BF16)
     chunk_home(tokdq, o_ddq, 17)
 
-    @pl.loop(G // 4, G // 2)
-    def _(n):
-        cross_grads(n)
-
     for k, ref in enumerate((o_eo, o_edq, o_edk, o_edv, o_do, o_ddq, o_cdk, o_cdv)):
         drain(ref, sem_out.at[k])
 
@@ -497,7 +527,8 @@
     drain(qt.at[0:NX * TC, :], sem_send.at[29])
     drain(nsend.at[0:NX], sem_send.at[30])
     drain(stat.at[0:NX], sem_send.at[31])
-    drain(qt.at[0:(NF - 1) * TC, :], sem_send.at[11])
+    drain(qt.at[0:(NX - 1) * TC, :], sem_send.at[11])
+    drain(qt.at[0:NX * TC, :], sem_send.at[32])
     drain(nsend.at[0:NX - 1], sem_send.at[12])
     drain(stat.at[0:NX - 1], sem_send.at[13])
     drain(stat.at[0:NF - 1], sem_send.at[18])
@@ -548,8 +579,8 @@
         v((HD, G * FB), BF16), v((HD, G * FB), BF16),
         v((NF * TC, HD), BF16), v((NF * TC, HD), BF16),
         v((G * FB, NF * TC), BF16), v((G * FB, NF * TC), BF16),
-        v((NW, 2 * FB), F32),
-        v((NW, 2 * FB), BF16), v((NW, 2 * FB), BF16),
+        v((NW, 2 * FB), F32), v((NW, 2 * FB), F32),
+        v((NW, 2 * FB), BF16), v((NW, 2 * FB), BF16), v((NW, 2 * FB), BF16),
         v((2 * G * FB, HD), F32),
         v((NF, HD, TC), BF16), v((NX, HD, TC), BF16),
         v((NF, HD, TC), BF16), v((NX, HD, TC), F32),
@@ -574,7 +605,7 @@
         pltpu.SemaphoreType.DMA((NF,)),
         pltpu.SemaphoreType.DMA((2,)),
         pltpu.SemaphoreType.DMA((8,)),
-        pltpu.SemaphoreType.DMA((32,)),
+        pltpu.SemaphoreType.DMA((33,)),
     ]
     shapes = (frames, frames, frames, frames, tokens, tokens, frames, frames)
     staged = pl.pallas_call(

time: 63.4 us -> 61.4 us (0.968)
  Pallas kernels: 62.6 us -> 60.4 us
    pallas_call x1, Pallas kernels: 60.3 us -> 58.1 us  [local(): pl.pallas_call(functools.partial(kernel, G, NF), out_shape=shapes, in_spe...]
where the time goes in v3:
time: 61.4 us; the launch traced here: 61.2 us
  Pallas kernels  60.4 us (98%)
  between operations  0.8 us (1%)
    pallas_call x1, Pallas kernels, local(): pl.pallas_call(functools.partial(kernel, G, NF), out_shape=shapes, in_spe...  58.1 us
    pallas_call x1, Pallas kernels, local(): pl.pallas_call(finish, out_shape=shapes, in_specs=[any_spec] * 8, out_spe...  2.27 us

profile of v3, /device:TPU:1, one launch (start us, length us, event | category | flops | bytes accessed | tf_op | source)
XLA Modules:
  0.0 61.2 jit_solution(7292271748510768005)
XLA Ops:
  0.6 58.1 %shard_map.152 = (bf16[128,1024]{1,0:T(8,128)(2,1)}, bf16[128,1024]{1,0:T(8,128)(2,1)}, bf16[128,1024]{1,0:T(8,128)(2,1)}, bf16[128,1024]{1,0:T(8,128)(2,1)}, bf...) custom-call(s32[64]{0:T(128)} %len_ref.1, ...), custom_call_target="tpu_custom_call" | custom-call | tf_op jit(solution)/shard_map/pallas_call | solution.py:611
  58.8 2.3 %shard_map.153 = (bf16[128,1024]{1,0:T(8,128)(2,1)}, bf16[128,1024]{1,0:T(8,128)(2,1)}, bf16[128,1024]{1,0:T(8,128)(2,1)}, bf16[128,1024]{1,0:T(8,128)(2,1)}, bf...) custom-call(bf16[128,1024]{1,0:T(8,128)(2,1)} %get-tuple-element.16.re, ...), custom_call_target="tpu_custom_call" | custom-call | tf_op jit(solution)/shard_map/pallas_call | solution.py:621

commit v4 on v3

--- a/solution.py
+++ b/solution.py
@@ -107,6 +107,27 @@
         greet(worker(fo, h), g)
         greet(f * G + r, g)
 
+    pl.semaphore_wait(barrier, 4 * G + NF - 1 - 2 * jnp.where(same, 1, 0))
+
+    place = r * 2 + g
+    own_tok = fo * (2 * G) + place
+
+    def tokens_out(src, dst, k):
+        for n in range(2 * G):
+            to = lax.rem(h * 2 + g + n, 2 * G)
+            th, tg = lax.div(to, 2), lax.rem(to, 2)
+            move(n, cols(src, tg * G + th), rows(dst, own_tok, TB), sem_send.at[k], sem_tok.at[k, fo], worker(fo, th), tg)
+
+    tokens_out(dqh, qt, 0)
+
+    def spread(src, dst, slot, ks, ki):
+        for n in range(G):
+            p = lax.rem(h + n, G)
+            move(n, cols(src, p), rows(dst, slot, FB), sem_send.at[ks], sem_in.at[ki], worker(fo, p), g)
+
+    spread(ckh, ckb, r, 2, 0)
+    spread(cvh, cvb, r, 3, 1)
+
     row = lax.broadcasted_iota(jnp.int32, (FB, HD), 0)
     for blk in range(2 * G):
         gb = f * G - R + blk
@@ -127,27 +148,6 @@
 
     eka[...] = jnp.zeros(eka.shape, F32)
     eva[...] = jnp.zeros(eva.shape, F32)
-
-    pl.semaphore_wait(barrier, 4 * G + NF - 1 - 2 * jnp.where(same, 1, 0))
-
-    place = r * 2 + g
-    own_tok = fo * (2 * G) + place
-
-    def tokens_out(src, dst, k):
-        for n in range(2 * G):
-            to = lax.rem(h * 2 + g + n, 2 * G)
-            th, tg = lax.div(to, 2), lax.rem(to, 2)
-            move(n, cols(src, tg * G + th), rows(dst, own_tok, TB), sem_send.at[k], sem_tok.at[k, fo], worker(fo, th), tg)
-
-    tokens_out(dqh, qt, 0)
-
-    def spread(src, dst, slot, ks, ki):
-        for n in range(G):
-            p = lax.rem(h + n, G)
-            move(n, cols(src, p), rows(dst, slot, FB), sem_send.at[ks], sem_in.at[ki], worker(fo, p), g)
-
-    spread(ckh, ckb, r, 2, 0)
-    spread(cvh, cvb, r, 3, 1)
 
     drain(rows(qt, f, TC), sem_tok.at[0, f])
     partner = worker(2 * x + 1 - c, h)
@@ -461,8 +461,9 @@
         drain(stat.at[t], sem_stat.at[t])
         return cross_backward(t)
 
-    @pl.loop(0, NX)
-    def _(i):
+    order = sorted(range(1, NX), key=lambda i: -min(i, NX - i))
+
+    for i in (*order, 0):
         t = other_core(i)
         drain(rows(ct, t, TC), sem_tok.at[1, t])
         dqsend[t] = backward_step(t).astype(BF16)
@@ -476,25 +477,30 @@
         send(dqsend.at[t], dqrecv.at[x], sem_send.at[21], sem_dq, worker(t, h), g)
 
     half_home(1 - back)
+
+    for i in order:
+        for_others(i)
+
     dqown[...] = cross_backward(f)
-
-    @pl.loop(1, NX - 1)
-    def _(i):
-        for_others(i)
-
     half_home(back)
-    for_others(NX - 1)
 
     def cross_grads(n):
-        u = lax.rem(z + n, G // 2)
-        here = pl.ds(pl.multiple_of(u * W, W), W)
+        here = pl.ds(pl.multiple_of(lax.rem(z + n, G // 2) * W, W), W)
         cdks[here, :] = (nn(dbuf[here, :], qt[...]) * SCALE).astype(BF16)
         cdvs[here, :] = nn(pbuf[here, :], ct[...]).astype(BF16)
+
+    def cross_home(n):
+        u = lax.rem(z + n, G // 2)
         for half in range(2):
             home(cdks, 2 * u + half, o_cdk, 24, 6)
             home(cdvs, 2 * u + half, o_cdv, 25, 7)
 
-    @pl.loop(0, G // 2)
+    @pl.loop(0, G // 4)
+    def _(n):
+        cross_grads(n)
+        cross_home(n)
+
+    @pl.loop(G // 4, G // 2)
     def _(n):
         cross_grads(n)
 
@@ -506,23 +512,26 @@
     tokdq[...] = (dq * SCALE).T.astype(BF16)
     chunk_home(tokdq, o_ddq, 17)
 
-    for k, ref in enumerate((o_eo, o_edq, o_edk, o_edv, o_do, o_ddq, o_cdk, o_cdv)):
-        drain(ref, sem_out.at[k])
-
-    def sent(kept):
-        for k in (2, 3, 4, 5, 6, 7, 14, 15, 22, 23, 24, 25):
+    @pl.loop(G // 4, G // 2)
+    def _(n):
+        cross_home(n)
+
+    def sent(kept, heads, tokens):
+        for k in heads:
             drain(eqb.at[0:(G - kept) * FB, :], sem_send.at[k])
-        for k in (0, 1, 16, 17):
+        for k in tokens:
             drain(qt.at[0:(2 * G - kept) * TB, :], sem_send.at[k])
 
-    @pl.when(same)
-    def _():
-        sent(1)
-
-    @pl.when(split)
-    def _():
-        sent(0)
-
+    def all_sent(heads, tokens):
+        @pl.when(same)
+        def _():
+            sent(1, heads, tokens)
+
+        @pl.when(split)
+        def _():
+            sent(0, heads, tokens)
+
+    all_sent((2, 3, 4, 5, 6, 7, 14, 15, 22, 23), (0, 1, 16))
     drain(qt.at[0:(NX - 1) * TC, :], sem_send.at[10])
     drain(qt.at[0:NX * TC, :], sem_send.at[29])
     drain(nsend.at[0:NX], sem_send.at[30])
@@ -546,6 +555,10 @@
         drain(rows(ekb, 0, R * FB), sem_send.at[26])
         drain(rows(evb, 0, R * FB), sem_send.at[27])
         drain(grecv.at[1], sem_send.at[20])
+
+    all_sent((24, 25), (17,))
+    for k, ref in enumerate((o_eo, o_edq, o_edk, o_edv, o_do, o_ddq, o_cdk, o_cdv)):
+        drain(ref, sem_out.at[k])
 
 
 def finish(*refs):

time: 61.4 us -> 60.5 us (0.985)
  Pallas kernels: 60.4 us -> 59.5 us
    pallas_call x1, Pallas kernels: 58.1 us -> 57.2 us  [local(): pl.pallas_call(functools.partial(kernel, G, NF), out_shape=shapes, in_spe...]
where the time goes in v4:
time: 60.5 us; the launch traced here: 60.3 us
  Pallas kernels  59.5 us (98%)
  between operations  0.8 us (1%)
    pallas_call x1, Pallas kernels, local(): pl.pallas_call(functools.partial(kernel, G, NF), out_shape=shapes, in_spe...  57.2 us
    pallas_call x1, Pallas kernels, local(): pl.pallas_call(finish, out_shape=shapes, in_specs=[any_spec] * 8, out_spe...  2.27 us

profile of v4, /device:TPU:1, one launch (start us, length us, event | category | flops | bytes accessed | tf_op | source)
XLA Modules:
  0.0 60.3 jit_solution(7115925947047750466)
XLA Ops:
  0.6 57.2 %shard_map.152 = (bf16[128,1024]{1,0:T(8,128)(2,1)}, bf16[128,1024]{1,0:T(8,128)(2,1)}, bf16[128,1024]{1,0:T(8,128)(2,1)}, bf16[128,1024]{1,0:T(8,128)(2,1)}, bf...) custom-call(s32[64]{0:T(128)} %len_ref.1, ...), custom_call_target="tpu_custom_call" | custom-call | tf_op jit(solution)/shard_map/pallas_call | solution.py:624
  57.9 2.3 %shard_map.153 = (bf16[128,1024]{1,0:T(8,128)(2,1)}, bf16[128,1024]{1,0:T(8,128)(2,1)}, bf16[128,1024]{1,0:T(8,128)(2,1)}, bf16[128,1024]{1,0:T(8,128)(2,1)}, bf...) custom-call(bf16[128,1024]{1,0:T(8,128)(2,1)} %get-tuple-element.16.re, ...), custom_call_target="tpu_custom_call" | custom-call | tf_op jit(solution)/shard_map/pallas_call | solution.py:634

commit v5 on v4

--- a/solution.py
+++ b/solution.py
@@ -330,19 +330,19 @@
         eka[pl.ds(at, W), :] += nn(ds, q)
         eva[pl.ds(at, W), :] += nn(prob.astype(BF16), cot)
 
-    def pair_step(j, sb, wb, inv, delta, nj, nsb, nwb):
+    def pair_step(j, sb, wb, inv, delta, nj, nsb, nwb, known):
         base = pl.multiple_of(j * W, W)
         top = None
         for u in range(NU):
             gradients(j, u, sb, inv, delta)
-            if nj is not None:
+            if nj is not None and known is None:
                 high = score(nj, u, nsb)
                 top = high if top is None else jnp.maximum(top, high)
         dq = nn(ekT[:, pl.ds(base, NU * W)], dsbuf[...]) * SCALE
         edqs[pl.ds(base, W), :] = dq.T.astype(BF16)
         ahead = None
         if nj is not None:
-            total = exponents(top, nsb, nwb)
+            total = exponents(top, nsb, nwb) if known is None else known
             ahead = output(nj, total, nwb)
         for half in range(2):
             home(eos, 2 * j + half, o_eo, 14, 0)
@@ -420,14 +420,19 @@
         high = score(pair_at(0), u, sbuf)
         top = high if top is None else jnp.maximum(top, high)
     total = exponents(top, sbuf, wbuf)
+    top = None
+    for u in range(NU):
+        high = score(pair_at(1), u, sbuf2)
+        top = high if top is None else jnp.maximum(top, high)
+    second = exponents(top, sbuf2, wbuf2)
     halo_in(1, evb)
     evT[...] = evb[...].T
     drain(ecb, sem_in.at[5])
+    ahead = output(pair_at(0), total, wbuf)
     drain(rows(ct, f, TC), sem_tok.at[1, f])
     for n in range(1, NX):
         send(rows(ct, f, TC), rows(ct, f, TC), sem_send.at[11], sem_tok.at[1, f], worker(same_core(n), h), g)
     send(rows(ct, f, TC), rows(ct, f, TC), sem_send.at[32], sem_tok.at[1, f], partner, g)
-    ahead = output(pair_at(0), total, wbuf)
     for i in range(G // 2):
         if i == G // 4:
             combine()
@@ -440,7 +445,7 @@
         more = i + 1 < G // 2
         ahead = pair_step(
             pair_at(i), *slots[i % 2], *ahead,
-            pair_at(i + 1) if more else None, *slots[(i + 1) % 2],
+            pair_at(i + 1) if more else None, *slots[(i + 1) % 2], second if i == 0 else None,
         )
 
     rim(1 - back)

time: 60.5 us -> 60.5 us (level)
  no operation moved by 1% of the time
where the time goes in v5:
time: 60.5 us; the launch traced here: 60.3 us
  Pallas kernels  59.5 us (98%)
  between operations  0.8 us (1%)
    pallas_call x1, Pallas kernels, local(): pl.pallas_call(functools.partial(kernel, G, NF), out_shape=shapes, in_spe...  57.2 us
    pallas_call x1, Pallas kernels, local(): pl.pallas_call(finish, out_shape=shapes, in_specs=[any_spec] * 8, out_spe...  2.27 us

profile of v5, /device:TPU:1, one launch (start us, length us, event | category | flops | bytes accessed | tf_op | source)
XLA Modules:
  0.0 60.3 jit_solution(15772550717959833619)
XLA Ops:
  0.6 57.2 %shard_map.152 = (bf16[128,1024]{1,0:T(8,128)(2,1)}, bf16[128,1024]{1,0:T(8,128)(2,1)}, bf16[128,1024]{1,0:T(8,128)(2,1)}, bf16[128,1024]{1,0:T(8,128)(2,1)}, bf...) custom-call(s32[64]{0:T(128)} %len_ref.1, ...), custom_call_target="tpu_custom_call" | custom-call | tf_op jit(solution)/shard_map/pallas_call | solution.py:629
  57.9 2.3 %shard_map.153 = (bf16[128,1024]{1,0:T(8,128)(2,1)}, bf16[128,1024]{1,0:T(8,128)(2,1)}, bf16[128,1024]{1,0:T(8,128)(2,1)}, bf16[128,1024]{1,0:T(8,128)(2,1)}, bf...) custom-call(bf16[128,1024]{1,0:T(8,128)(2,1)} %get-tuple-element.16.re, ...), custom_call_target="tpu_custom_call" | custom-call | tf_op jit(solution)/shard_map/pallas_call | solution.py:639
